TPU v7x, 32 devices: a whole 2x2x4 slice. The times are simulated.
32 devices in a mesh: dp: 8 (over z, y), blk: 4 (over x, core).
Axes of the slice: x: 2, y: 2, z: 4, core: 2. Of those that a mesh axis runs over, the one named last changes fastest.
Arguments:
- tokens: bfloat16 [8, 512, 768], P('dp', 'blk'), may hold values from -6 to 6
- early_gain: bfloat16 [768], replicated, may hold values from 0.5 to 1.5
- early_shift: bfloat16 [768], replicated, may hold values from -4 to 4
- query_weight: bfloat16 [768, 768], replicated, may hold values from -0.21875 to 0.21875
- query_bias: bfloat16 [768], replicated, may hold values from -4 to 4
- key_weight: bfloat16 [768, 768], replicated, may hold values from -0.21875 to 0.21875
- value_weight: bfloat16 [768, 768], replicated, may hold values from -0.21875 to 0.21875
- value_bias: bfloat16 [768], replicated, may hold values from -0.75 to 0.75
- output_weight: bfloat16 [768, 768], replicated, may hold values from -2.5 to 2.5
- output_bias: bfloat16 [768], replicated, may hold values from -4 to 4
- late_gain: bfloat16 [768], replicated, may hold values from 0.5 to 1.5
- late_shift: bfloat16 [768], replicated, may hold values from -4 to 4
- expand_weight: bfloat16 [768, 3072], replicated, may hold values from -0.21875 to 0.21875
- expand_bias: bfloat16 [3072], replicated, may hold values from -4 to 4
- contract_weight: bfloat16 [3072, 768], replicated, may hold values from -0.109375 to 0.109375
- contract_bias: bfloat16 [768], replicated, may hold values from -4 to 4
- upstream: bfloat16 [8, 512, 768], P('dp', 'blk'), may hold values from -6 to 6
- clip_ids: int32 [8, 512], P('dp'), may hold values from 0 to 3, never falling along the last dimension, each value on 1 to 256 neighbouring positions
- block_order: int32 [8, 4], P('dp'), may hold values from 0 to 3, each once within a row
Outputs:
- block_out: bfloat16 [8, 512, 768], P('dp', 'blk')
- token_grad: bfloat16 [8, 512, 768], P('dp', 'blk')
- gain_early: float32 [768], P('dp')
- shift_early: float32 [768], P('dp')
- query_grad: float32 [768, 768], P('dp')
- bias_query: float32 [768], P('dp')
- key_grad: float32 [768, 768], P('dp')
- value_grad: float32 [768, 768], P('dp')
- bias_value: float32 [768], P('dp')
- output_grad: float32 [768, 768], P('dp')
- bias_output: float32 [768], P('dp')
- gain_late: float32 [768], P('dp')
- shift_late: float32 [768], P('dp')
- expand_grad: float32 [768, 3072], P('dp')
- bias_expand: float32 [3072], P('dp')
- contract_grad: float32 [3072, 768], P('dp')
- bias_contract: float32 [768], P('dp')
Inputs may be any that keep to these rules, and one draw needn't show every extreme that they name: `clip_ids`: along the logical positions of each row the clip number never falls; every row holds clips 0 to 3, each of 1 to 256 tokens, and in each row one clip has exactly 256. Each row is a permutation of 0 to 3; index j of blk holds, of each of its rows, the 128 tokens of logical positions block_order[row, j] * 128 onward.
All inputs are finite; a program needn't handle non-finite values.
Results may differ from a plain program's by a relative error of at most 0.02.
Values may be sent and summed in bfloat16 or wider, within the bound.
A program may use at most 192 MiB of HBM per device.

v0:
```python
import jax
import jax.numpy as jnp
from jax import lax
from jax.sharding import PartitionSpec as P

HEADS = 12


EPSILON = 1e-05
MASKED = -1e30


def passed_along(value, axis, steps):
    count = lax.axis_size(axis)
    pairs = [(source, (source + steps) % count) for source in range(count)]
    return lax.ppermute(value, axis, pairs)


def layer_norm(inputs, gain, shift):
    average = jnp.mean(inputs, axis=-1, keepdims=True)
    centred = inputs - average
    inverse = lax.rsqrt(jnp.mean(centred * centred, axis=-1, keepdims=True) + EPSILON)
    normed = centred * inverse
    return (normed * gain + shift, normed, inverse)


def norm_back(grad_out, normed, inverse, gain):
    scaled = grad_out * gain
    inner = (
        scaled
        - jnp.mean(scaled, axis=-1, keepdims=True)
        - normed * jnp.mean(scaled * normed, axis=-1, keepdims=True)
    )
    return (
        inverse * inner,
        jnp.sum(grad_out * normed, axis=(0, 1)),
        jnp.sum(grad_out, axis=(0, 1)),
    )


def project(inputs, weight):
    return jnp.einsum("rtd,de->rte", inputs, weight, preferred_element_type=jnp.float32)


def project_back(grad_rows, weight):
    return jnp.einsum("rte,de->rtd", grad_rows, weight, preferred_element_type=jnp.float32)


def weight_grad(inputs, grad_rows):
    return jnp.einsum("rtd,rte->de", inputs, grad_rows, preferred_element_type=jnp.float32)


def column_sum(grad_rows):
    return jnp.sum(grad_rows.astype(jnp.float32), axis=(0, 1))


def local(
    tokens,
    early_gain,
    early_shift,
    query_weight,
    query_bias,
    key_weight,
    value_weight,
    value_bias,
    output_weight,
    output_bias,
    late_gain,
    late_shift,
    expand_weight,
    expand_bias,
    contract_weight,
    contract_bias,
    upstream,
    clip_ids,
    block_order,
):
    row_count, block_len, features = tokens.shape
    head_count = HEADS
    head_size = features // head_count
    scale_factor = float(head_size) ** (-0.5)
    my_index = lax.axis_index("blk")
    group_size = lax.axis_size("blk")

    def positions(begin, length):
        stored = begin + jnp.arange(length, dtype=jnp.int32)
        logical = (
            jnp.take(block_order, stored // block_len, axis=1) * block_len + stored % block_len
        )
        return (logical, jnp.take_along_axis(clip_ids, logical, axis=1))

    query_pos, query_clip = positions(my_index * block_len, block_len)

    def visible(begin, length):
        key_pos, key_clip = positions(begin, length)
        allowed = (key_pos[:, None, :] <= query_pos[:, :, None]) & (
            key_clip[:, None, :] == query_clip[:, :, None]
        )
        return allowed[:, None]

    def split_heads(array):
        return array.reshape(row_count, array.shape[1], head_count, head_size)

    inputs = tokens.astype(jnp.float32)
    first_full, first_normed, first_inverse = layer_norm(
        inputs, early_gain.astype(jnp.float32), early_shift.astype(jnp.float32)
    )
    first_low = first_full.astype(jnp.bfloat16)
    queries = (project(first_low, query_weight) + query_bias.astype(jnp.float32)).astype(
        jnp.bfloat16
    )
    key_rows = project(first_low, key_weight).astype(jnp.bfloat16)
    value_rows = (project(first_low, value_weight) + value_bias.astype(jnp.float32)).astype(
        jnp.bfloat16
    )
    query_heads = split_heads(queries)

    def scores_of(key_block):
        return (
            jnp.einsum(
                "rqhe,rkhe->rhqk",
                query_heads,
                split_heads(key_block),
                preferred_element_type=jnp.float32,
            )
            * scale_factor
        )

    def absorb(carry, key_block, value_block, begin):
        allowed = visible(begin, key_block.shape[1])
        maximum, denominator, numerator = carry
        scores = jnp.where(allowed, scores_of(key_block), MASKED)
        new_max = jnp.maximum(maximum, jnp.max(scores, axis=-1))
        weights = jnp.where(allowed, jnp.exp(scores - new_max[..., None]), 0.0)
        factor = jnp.exp(maximum - new_max)
        update = jnp.einsum(
            "rhqk,rkhe->rqhe",
            weights.astype(jnp.bfloat16),
            split_heads(value_block),
            preferred_element_type=jnp.float32,
        )
        numerator = numerator * jnp.transpose(factor, (0, 2, 1))[..., None] + update
        return (new_max, denominator * factor + jnp.sum(weights, axis=-1), numerator)

    start_state = (
        jnp.full((row_count, head_count, block_len), MASKED, jnp.float32),
        jnp.zeros((row_count, head_count, block_len), jnp.float32),
        jnp.zeros((row_count, block_len, head_count, head_size), jnp.float32),
    )
    key_piece = lax.all_gather(key_rows, "blk", axis=1, tiled=True)
    value_piece = lax.all_gather(value_rows, "blk", axis=1, tiled=True)
    length = key_piece.shape[1]
    stride = min(length, block_len)

    def one_block(number, running):
        offset = number * stride
        return absorb(
            running,
            lax.dynamic_slice_in_dim(key_piece, offset, stride, 1),
            lax.dynamic_slice_in_dim(value_piece, offset, stride, 1),
            offset,
        )

    maximum, denominator, numerator = lax.fori_loop(0, length // stride, one_block, start_state)
    log_total = maximum + jnp.log(denominator)
    attention = numerator / jnp.transpose(denominator, (0, 2, 1))[..., None]
    attention_low = attention.reshape(row_count, block_len, features).astype(jnp.bfloat16)
    middle = inputs + project(attention_low, output_weight) + output_bias.astype(jnp.float32)
    second_full, second_normed, second_inverse = layer_norm(
        middle, late_gain.astype(jnp.float32), late_shift.astype(jnp.float32)
    )
    second_low = second_full.astype(jnp.bfloat16)
    hidden = project(second_low, expand_weight) + expand_bias.astype(jnp.float32)
    active_full, gelu_pull = jax.vjp(
        lambda values_in: jax.nn.gelu(values_in, approximate=True), hidden
    )
    active_low = active_full.astype(jnp.bfloat16)
    block_out = (
        middle + project(active_low, contract_weight) + contract_bias.astype(jnp.float32)
    ).astype(jnp.bfloat16)
    grad_out = upstream.astype(jnp.float32)
    contract_g = weight_grad(active_low, upstream)
    contract_b = column_sum(upstream)
    hidden_low = gelu_pull(project_back(upstream, contract_weight))[0].astype(jnp.bfloat16)
    expand_g = weight_grad(second_low, hidden_low)
    expand_b = column_sum(hidden_low)
    norm_grad, late_gain_g, late_shift_g = norm_back(
        project_back(hidden_low, expand_weight),
        second_normed,
        second_inverse,
        late_gain.astype(jnp.float32),
    )
    middle_grad = grad_out + norm_grad
    branch_low = middle_grad.astype(jnp.bfloat16)
    output_g = weight_grad(attention_low, branch_low)
    output_b = column_sum(branch_low)
    grad_heads = split_heads(project_back(branch_low, output_weight).astype(jnp.bfloat16))
    delta = jnp.transpose(jnp.sum(grad_heads.astype(jnp.float32) * attention, axis=-1), (0, 2, 1))

    def turn_step(number, carried):
        key_block, value_block, key_acc, value_acc, query_acc = carried
        source = (my_index - number) % group_size
        allowed = visible(source * block_len, block_len)
        use_key, use_value = (key_block, value_block)
        key_sum = key_acc
        value_sum = value_acc
        query_sum = query_acc
        probs = jnp.where(allowed, jnp.exp(scores_of(use_key) - log_total[..., None]), 0.0)
        value_sum = value_sum + jnp.einsum(
            "rhqk,rqhe->rkhe",
            probs.astype(jnp.bfloat16),
            grad_heads,
            preferred_element_type=jnp.float32,
        ).reshape(row_count, block_len, features)
        prob_grad = jnp.einsum(
            "rqhe,rkhe->rhqk",
            grad_heads,
            split_heads(use_value),
            preferred_element_type=jnp.float32,
        )
        score_grad = (probs * (prob_grad - delta[..., None])).astype(jnp.bfloat16)
        query_sum = (
            query_sum
            + jnp.einsum(
                "rhqk,rkhe->rqhe",
                score_grad,
                split_heads(use_key),
                preferred_element_type=jnp.float32,
            )
            * scale_factor
        )
        key_sum = key_sum + (
            jnp.einsum(
                "rhqk,rqhe->rkhe", score_grad, query_heads, preferred_element_type=jnp.float32
            )
            * scale_factor
        ).reshape(row_count, block_len, features)
        key_acc = key_sum
        value_acc = value_sum
        key_block, value_block = passed_along((key_block, value_block), "blk", 1)
        key_acc, value_acc = (
            passed_along(key_acc.astype(jnp.bfloat16), "blk", 1).astype(key_acc.dtype),
            passed_along(value_acc.astype(jnp.bfloat16), "blk", 1).astype(value_acc.dtype),
        )
        return (key_block, value_block, key_acc, value_acc, query_sum)

    zero_rows = jnp.zeros((row_count, block_len, features), jnp.float32)
    carried = (
        key_rows,
        value_rows,
        zero_rows,
        zero_rows,
        jnp.zeros((row_count, block_len, head_count, head_size), jnp.float32),
    )
    carried = lax.fori_loop(0, group_size, turn_step, carried)
    query_low = carried[4].reshape(row_count, block_len, features).astype(jnp.bfloat16)
    key_low = carried[2].astype(jnp.bfloat16)
    value_low = carried[3].astype(jnp.bfloat16)
    query_g = weight_grad(first_low, query_low)
    key_g = weight_grad(first_low, key_low)
    value_g = weight_grad(first_low, value_low)
    query_b = column_sum(query_low)
    value_b = column_sum(value_low)
    first_grad = (
        project_back(query_low, query_weight)
        + project_back(key_low, key_weight)
        + project_back(value_low, value_weight)
    )
    input_grad, early_gain_g, early_shift_g = norm_back(
        first_grad, first_normed, first_inverse, early_gain.astype(jnp.float32)
    )
    token_grad = (middle_grad + input_grad).astype(jnp.bfloat16)
    local_grads = (
        early_gain_g,
        early_shift_g,
        query_g,
        query_b,
        key_g,
        value_g,
        value_b,
        output_g,
        output_b,
        late_gain_g,
        late_shift_g,
        expand_g,
        expand_b,
        contract_g,
        contract_b,
    )
    owners = lax.axis_size("dp")
    laid_out = jnp.concatenate([member.reshape(owners, -1) for member in local_grads], axis=1)
    shares = lax.psum_scatter(laid_out.astype(jnp.bfloat16), "dp", scatter_dimension=0, tiled=True)
    summed = lax.psum(shares, "blk").astype(jnp.float32)
    pieces = []
    offset = 0
    for member in local_grads:
        width = member.size // owners
        own_shape = (member.shape[0] // owners,) + member.shape[1:]
        pieces.append(summed[0, offset : offset + width].reshape(own_shape))
        offset = offset + width
    return (block_out, token_grad) + tuple(pieces)


def solution(mesh):
    placed = (
        P("dp", "blk", None),
        P(),
        P(),
        P(),
        P(),
        P(),
        P(),
        P(),
        P(),
        P(),
        P(),
        P(),
        P(),
        P(),
        P(),
        P(),
        P("dp", "blk", None),
        P("dp", None),
        P("dp", None),
    )
    return jax.shard_map(
        local,
        mesh=mesh,
        in_specs=placed,
        out_specs=(
            P("dp", "blk", None),
            P("dp", "blk", None),
            P("dp"),
            P("dp"),
            P("dp", None),
            P("dp"),
            P("dp", None),
            P("dp", None),
            P("dp"),
            P("dp", None),
            P("dp"),
            P("dp"),
            P("dp"),
            P("dp", None),
            P("dp"),
            P("dp", None),
            P("dp"),
        ),
        check_vma=False,
    )
```

profile of v0, /device:TPU:3, one launch (start us, length us, event | category | flops | bytes accessed | tf_op | source)
XLA Modules:
  0.0 874.7 jit_solution(15544935418907451147)
XLA Ops:
  10.2 3.1 fusion.96
  17.5 1.8 convolution_convert_fusion.7
  19.3 9.2 %all-gather = bf16[512,768]{1,0:T(8,128)(2,1)} all-gather(bf16[128,768]{1,0:T(8,128)(2,1)S(1)} %convolution_convert_fusion.7), channel_id=2, replica_groups=mesh['dp'=8,'blk'=4] {'blk'}, dimensions={0}, use_global_device_ids=true | all-gather | bytes 983040 | tf_op jit(solution)/shard_map/all_gather | solution.py:150
  32.5 9.2 %all-gather.1 = bf16[512,768]{1,0:T(8,128)(2,1)} all-gather(bf16[128,768]{1,0:T(8,128)(2,1)S(1)} %fusion.52), channel_id=3, replica_groups=mesh['dp'=8,'blk'=4] {'blk'}, dimensions={0}, use_global_device_ids=true | all-gather | bytes 983040 | tf_op jit(solution)/shard_map/all_gather | solution.py:151
  43.1 33.3 %while.45 = (s32[]{:T(128)}, f32[1,12,128]{2,1,0:T(8,128)S(1)}, f32[1,12,128]{2,1,0:T(8,128)S(1)}, f32[1,128,12,64]{1,3,2,0:T(8,128)}, s32[1,4]{1,0:T(1,128)S(1)...) while((s32[]{:T(128)}, f32[1,12,128]{2,1,0:T(8,128)S(1)}, ...), condition=%wide.region_5.8_spmd.clone, body=%wide.region_2.7_spmd.clone.sunk | while | flops 52462216 | bytes 5483271 | solution.py:164
  45.0 2.6 fusion.177
  52.6 2.6 fusion.177
  57.3 2.0 fusion.182
  61.1 2.6 fusion.177
  65.9 2.0 fusion.182
  69.7 2.6 fusion.177
  74.4 2.0 fusion.182
  77.6 1.8 fusion.116
  79.7 3.3 convolution_add_fusion
  83.1 5.5 fusion.117
  88.6 2.3 fusion.68
  93.9 2.1 convert_reduce_fusion.2
  99.0 75.8 %while.46 = (s32[]{:T(128)}, bf16[1,128,768]{1,2,0:T(8,128)(2,1)}, bf16[1,128,768]{1,2,0:T(8,128)(2,1)}, f32[1,128,768]{1,2,0:T(8,128)S(1)}, f32[1,128,768]{1,2,...) while((s32[]{:T(128)}, bf16[1,128,768]{1,2,0:T(8,128)(2,1)}, ...), condition=%wide.region_12.15_spmd.clone, body=%wide.region_11.14_spmd.clone.sunk | while | flops 128442000 | bytes 13646902 | solution.py:255
  102.5 2.6 fusion.194
  117.6 2.5 collective-permute-start
  121.6 2.6 fusion.194
  130.9 2.1 fusion.201
  136.9 2.5 collective-permute-start
  140.9 2.6 fusion.194
  150.3 2.1 fusion.201
  156.3 2.5 collective-permute-start
  160.3 2.6 fusion.194
  169.5 2.1 fusion.201
  176.2 1.8 fusion.118
  183.0 3.6 convolution_convert_fusion.1
  186.7 3.8 convolution_convert_fusion
  193.7 2.8 reshape.925
  196.6 2.9 reshape.927
  201.2 1.8 reshape.930
  203.2 6.7 reshape.934
  210.0 17.0 %reshape.936 = bf16[8,294912]{1,0:T(8,128)(2,1)} reshape(bf16[3072,768]{1,0:T(8,128)(2,1)} %convolution_convert_fusion) | data formatting | bytes 9437184 | tf_op jit(solution)/shard_map/reshape | solution.py:291
  229.8 7.7 dynamic-update-slice.2
  239.0 7.7 dynamic-update-slice.4
  246.7 7.7 dynamic-update-slice.5
  261.1 25.6 %dynamic-update-slice.11 = bf16[8,885888]{1,0:T(8,128)(2,1)} dynamic-update-slice(bf16[8,885888]{1,0:T(8,128)(2,1)} %dynamic-update-slice.10, bf16[8,294912]{1,0:T(8,128)(2,1)} %reshape.934, s32[]{} %constant.363, s32[]{} %constant.374) | dynamic-update-slice | bytes 9437188
  288.2 25.3 %dynamic-update-slice.13 = bf16[8,885888]{1,0:T(8,128)(2,1)} dynamic-update-slice(bf16[8,885888]{1,0:T(8,128)(2,1)} %dynamic-update-slice.12, bf16[8,294912]{1,0:T(8,128)(2,1)} %reshape.936, s32[]{} %constant.363, s32[]{} %constant.376) | dynamic-update-slice | bytes 9437188
  315.9 440.9 %all-reduce.6.cloned.1.call-done = bf16[8,885888]{1,0:T(8,128)(2,1)} async-done(((bf16[8,885888]{1,0:T(8,128)(2,1)}), bf16[8,885888]{1,0:T(8,128)(2,1)}) %all-reduce.6.cloned.1.call-update) | async-done | bytes 14174224
  756.8 8.8 %constant_dynamic-slice_fusion.2 = bf16[1,885888]{1,0:T(2,128)(2,1)} fusion(bf16[8,885888]{1,0:T(8,128)(2,1)} %all-reduce.6.cloned.1.call-done, u32[]{:T(128)} %bitcast.96), kind=kLoop, calls=%fused_computation.202 | loop fusion | bytes 3543556
  766.5 4.6 fusion.50
  771.1 68.1 %all-reduce.4.cloned.1.call-done = bf16[1,885888]{1,0:T(2,128)(2,1)} async-done(((bf16[1,885888]{1,0:T(2,128)(2,1)}), bf16[1,885888]{1,0:T(2,128)(2,1)}) %all-reduce.4.cloned.1.call-update) | async-done | bytes 1771792 | tf_op jit(solution)/shard_map/psum | solution.py:293
  839.2 6.3 convert_element_type.254
  846.1 2.9 slice_reduce_fusion.2
  849.0 12.5 %slice_reduce_fusion = (f32[294912]{0:T(1024)S(1)}, f32[294912]{0:T(1024)S(1)}) fusion(f32[1,885888]{1,0:T(1,128)S(1)} %convert_element_type.254), kind=kLoop, calls=%fused_computation.116 | loop fusion | bytes 4718592 | tf_op jit(solution)/shard_map/slice | solution.py:299
  (358 shorter events, 121.2 us)
Async XLA Ops:
  7.2 24.2 %copy-start = (bf16[768,768]{1,0:T(8,128)(2,1)S(1)}, bf16[768,768]{1,0:T(8,128)(2,1)}, u32[]{:S(2)}) copy-start(bf16[768,768]{1,0:T(8,128)(2,1)} %param.33) | copy-start | bytes 3538948
  7.2 21.3 %copy-start.4 = (bf16[1,128,768]{2,1,0:T(8,128)(2,1)S(1)}, bf16[1,128,768]{2,1,0:T(8,128)(2,1)}, u32[]{:S(2)}) copy-start(bf16[1,128,768]{2,1,0:T(8,128)(2,1)} %param.27) | copy-start | bytes 589828
  7.2 21.3 %copy-start.17 = (bf16[768,768]{1,0:T(8,128)(2,1)S(1)}, bf16[768,768]{1,0:T(8,128)(2,1)}, u32[]{:S(2)}) copy-start(bf16[768,768]{1,0:T(8,128)(2,1)} %param.30) | copy-start | bytes 3538948
  7.2 749.6 %all-reduce.6.cloned.1.call-start = ((), (), s32[]{:S(2)}) async-start(), calls=%async_computation.1 | async-start | bytes 28348416
  10.2 18.3 %copy-start.55 = (bf16[768]{0:T(1024)(128)(2,1)S(1)}, bf16[768]{0:T(1024)(128)(2,1)}, u32[]{:S(2)}) copy-start(bf16[768]{0:T(1024)(128)(2,1)} %param.31) | copy-start | bytes 4612
  14.6 15.0 %copy-start.37 = (f32[768]{0:T(1024)}, f32[768]{0:T(1024)S(1)}, u32[]{:S(2)}) copy-start(f32[768]{0:T(1024)S(1)} %convert_element_type.221) | copy-start | bytes 9220
  15.3 13.2 %copy-start.33 = (f32[768]{0:T(1024)}, f32[768]{0:T(1024)S(1)}, u32[]{:S(2)}) copy-start(f32[768]{0:T(1024)S(1)} %convert_element_type.220) | copy-start | bytes 9220
  16.3 12.1 %copy-start.41 = (f32[128]{0:T(128)}, f32[128]{0:T(128)S(1)}, u32[]{:S(2)}) copy-start(f32[128]{0:T(128)S(1)} %broadcast_multiply_fusion.5) | copy-start | bytes 1540
  17.5 11.0 %copy-start.45 = (f32[128]{0:T(128)}, f32[128]{0:T(128)S(1)}, u32[]{:S(2)}) copy-start(f32[128]{0:T(128)S(1)} %add_rsqrt_fusion.1) | copy-start | bytes 1540
  19.2 9.2 %copy-start.20 = (bf16[128,768]{1,0:T(8,128)(2,1)}, bf16[128,768]{1,0:T(8,128)(2,1)S(1)}, u32[]{:S(2)}) copy-start(bf16[128,768]{1,0:T(8,128)(2,1)S(1)} %convolution_convert_fusion.7) | copy-start | bytes 589828
  29.6 12.1 %copy-start.2 = (s32[1,512]{1,0:T(1,128)S(1)}, s32[1,512]{1,0:T(1,128)}, u32[]{:S(2)}) copy-start(s32[1,512]{1,0:T(1,128)} %param.44) | copy-start | bytes 6148
  31.4 11.7 %copy-start.39 = (s32[1,128]{1,0:T(1,128)S(1)}, s32[1,128]{1,0:T(1,128)}, u32[]{:S(2)}) copy-start(s32[1,128]{1,0:T(1,128)} %get-tuple-element.1216) | copy-start | bytes 1540
  31.4 11.7 %copy-start.19 = (s32[1,4]{1,0:T(1,128)S(1)}, s32[1,4]{1,0:T(1,128)}, u32[]{:S(2)}) copy-start(s32[1,4]{1,0:T(1,128)} %param.45) | copy-start | bytes 52
  31.4 11.7 %copy-start.26 = (f32[1,12,128]{2,1,0:T(8,128)S(1)}, f32[1,12,128]{2,1,0:T(8,128)}, u32[]{:S(2)}) copy-start(f32[1,12,128]{2,1,0:T(8,128)} %custom-call.1) | copy-start | bytes 18436
  32.5 10.7 %copy-start.22 = (bf16[128,768]{1,0:T(8,128)(2,1)}, bf16[128,768]{1,0:T(8,128)(2,1)S(1)}, u32[]{:S(2)}) copy-start(bf16[128,768]{1,0:T(8,128)(2,1)S(1)} %fusion.52) | copy-start | bytes 589828
  43.1 33.4 %copy-start.54 = (bf16[3072]{0:T(1024)(128)(2,1)S(1)}, bf16[3072]{0:T(1024)(128)(2,1)}, u32[]{:S(2)}) copy-start(bf16[3072]{0:T(1024)(128)(2,1)} %param.40) | copy-start | bytes 18436
  43.1 33.4 %copy-start.56 = (bf16[768]{0:T(1024)(128)(2,1)S(1)}, bf16[768]{0:T(1024)(128)(2,1)}, u32[]{:S(2)}) copy-start(bf16[768]{0:T(1024)(128)(2,1)} %param.38) | copy-start | bytes 4612
  43.1 33.4 %copy-start.57 = (bf16[768]{0:T(1024)(128)(2,1)S(1)}, bf16[768]{0:T(1024)(128)(2,1)}, u32[]{:S(2)}) copy-start(bf16[768]{0:T(1024)(128)(2,1)} %param.37) | copy-start | bytes 4612
  76.5 6.5 copy-start.35
  76.5 14.4 %copy-start.30 = (f32[768]{0:T(1024)}, f32[768]{0:T(1024)S(1)}, u32[]{:S(2)}) copy-start(f32[768]{0:T(1024)S(1)} %convert_element_type.233) | copy-start | bytes 9220
  79.4 9.1 %copy-start.43 = (f32[128]{0:T(128)}, f32[128]{0:T(128)S(1)}, u32[]{:S(2)}) copy-start(f32[128]{0:T(128)S(1)} %broadcast_multiply_fusion.4) | copy-start | bytes 1540
  79.6 8.9 %copy-start.47 = (f32[128]{0:T(128)}, f32[128]{0:T(128)S(1)}, u32[]{:S(2)}) copy-start(f32[128]{0:T(128)S(1)} %add_rsqrt_fusion) | copy-start | bytes 1540
  79.7 8.9 %slice-start = ((s8[4718592]{0:T(1024)(128)(4,1)}), s8[4194304]{0:T(1024)(128)(4,1)S(1)}, s32[]{:S(2)}) async-start(s8[4718592]{0:T(1024)(128)(4,1)} %bitcast.369), calls=%async_computation.2 | async-start | bytes 8388608
  83.1 5.5 copy-start.6
  83.1 5.5 slice-start.1
  99.0 9.3 %copy-start.32 = (f32[1,12,128]{2,1,0:T(8,128)S(1)}, f32[1,12,128]{2,1,0:T(8,128)}, u32[]{:S(2)}) copy-start(f32[1,12,128]{2,1,0:T(8,128)} %get-tuple-element.1262) | copy-start | bytes 18436 | tf_op jit(solution)/shard_map/while
  100.0 16.7 %collective-permute-start = (bf16[1,128,768]{1,2,0:T(8,128)(2,1)S(1)}, bf16[1,128,768]{1,2,0:T(8,128)(2,1)}, u32[]{:S(2)}, u32[]{:S(2)}) collective-permute-start(bf16[1,128,768]{1,2,0:T(8,128)(2,1)S(1)} %copy.85), channel_id=1, source_target_pairs={{0,1},{1,2},{2,3},{3,0},{4,5},{5,6},{6,7},{7,4},{8,9},{9,10},{10,1... | collective-permute-start | bytes 589832 | tf_op jit(solution)/shard_map/while/body/eval_jaxpr/ppermute | solution.py:16
  101.6 15.1 %collective-permute-start.1 = (bf16[1,128,768]{1,2,0:T(8,128)(2,1)S(1)}, bf16[1,128,768]{1,2,0:T(8,128)(2,1)}, u32[]{:S(2)}, u32[]{:S(2)}) collective-permute-start(bf16[1,128,768]{1,2,0:T(8,128)(2,1)S(1)} %copy.86), channel_id=1, source_target_pairs={{0,1},{1,2},{2,3},{3,0},{4,5},{5,6},{6,7},{7,4},{8,9},{9,10},{10,1... | collective-permute-start | bytes 589832 | tf_op jit(solution)/shard_map/while/body/eval_jaxpr/ppermute | solution.py:16
  109.8 3.8 collective-permute-start.2
  111.6 4.1 collective-permute-start.3
  116.7 10.8 %copy-start.32 = (f32[1,12,128]{2,1,0:T(8,128)S(1)}, f32[1,12,128]{2,1,0:T(8,128)}, u32[]{:S(2)}) copy-start(f32[1,12,128]{2,1,0:T(8,128)} %get-tuple-element.1262) | copy-start | bytes 18436 | tf_op jit(solution)/shard_map/while
  117.6 18.3 %collective-permute-start = (bf16[1,128,768]{1,2,0:T(8,128)(2,1)S(1)}, bf16[1,128,768]{1,2,0:T(8,128)(2,1)}, u32[]{:S(2)}, u32[]{:S(2)}) collective-permute-start(bf16[1,128,768]{1,2,0:T(8,128)(2,1)S(1)} %copy.85), channel_id=1, source_target_pairs={{0,1},{1,2},{2,3},{3,0},{4,5},{5,6},{6,7},{7,4},{8,9},{9,10},{10,1... | collective-permute-start | bytes 589832 | tf_op jit(solution)/shard_map/while/body/eval_jaxpr/ppermute | solution.py:16
  121.0 14.9 %collective-permute-start.1 = (bf16[1,128,768]{1,2,0:T(8,128)(2,1)S(1)}, bf16[1,128,768]{1,2,0:T(8,128)(2,1)}, u32[]{:S(2)}, u32[]{:S(2)}) collective-permute-start(bf16[1,128,768]{1,2,0:T(8,128)(2,1)S(1)} %copy.86), channel_id=1, source_target_pairs={{0,1},{1,2},{2,3},{3,0},{4,5},{5,6},{6,7},{7,4},{8,9},{9,10},{10,1... | collective-permute-start | bytes 589832 | tf_op jit(solution)/shard_map/while/body/eval_jaxpr/ppermute | solution.py:16
  128.8 4.1 collective-permute-start.2
  130.9 4.1 collective-permute-start.3
  135.9 10.8 %copy-start.32 = (f32[1,12,128]{2,1,0:T(8,128)S(1)}, f32[1,12,128]{2,1,0:T(8,128)}, u32[]{:S(2)}) copy-start(f32[1,12,128]{2,1,0:T(8,128)} %get-tuple-element.1262) | copy-start | bytes 18436 | tf_op jit(solution)/shard_map/while
  136.9 18.5 %collective-permute-start = (bf16[1,128,768]{1,2,0:T(8,128)(2,1)S(1)}, bf16[1,128,768]{1,2,0:T(8,128)(2,1)}, u32[]{:S(2)}, u32[]{:S(2)}) collective-permute-start(bf16[1,128,768]{1,2,0:T(8,128)(2,1)S(1)} %copy.85), channel_id=1, source_target_pairs={{0,1},{1,2},{2,3},{3,0},{4,5},{5,6},{6,7},{7,4},{8,9},{9,10},{10,1... | collective-permute-start | bytes 589832 | tf_op jit(solution)/shard_map/while/body/eval_jaxpr/ppermute | solution.py:16
  140.3 15.1 %collective-permute-start.1 = (bf16[1,128,768]{1,2,0:T(8,128)(2,1)S(1)}, bf16[1,128,768]{1,2,0:T(8,128)(2,1)}, u32[]{:S(2)}, u32[]{:S(2)}) collective-permute-start(bf16[1,128,768]{1,2,0:T(8,128)(2,1)S(1)} %copy.86), channel_id=1, source_target_pairs={{0,1},{1,2},{2,3},{3,0},{4,5},{5,6},{6,7},{7,4},{8,9},{9,10},{10,1... | collective-permute-start | bytes 589832 | tf_op jit(solution)/shard_map/while/body/eval_jaxpr/ppermute | solution.py:16
  148.1 4.3 collective-permute-start.2
  150.3 4.1 collective-permute-start.3
  155.3 10.8 %copy-start.32 = (f32[1,12,128]{2,1,0:T(8,128)S(1)}, f32[1,12,128]{2,1,0:T(8,128)}, u32[]{:S(2)}) copy-start(f32[1,12,128]{2,1,0:T(8,128)} %get-tuple-element.1262) | copy-start | bytes 18436 | tf_op jit(solution)/shard_map/while
  156.3 18.3 %collective-permute-start = (bf16[1,128,768]{1,2,0:T(8,128)(2,1)S(1)}, bf16[1,128,768]{1,2,0:T(8,128)(2,1)}, u32[]{:S(2)}, u32[]{:S(2)}) collective-permute-start(bf16[1,128,768]{1,2,0:T(8,128)(2,1)S(1)} %copy.85), channel_id=1, source_target_pairs={{0,1},{1,2},{2,3},{3,0},{4,5},{5,6},{6,7},{7,4},{8,9},{9,10},{10,1... | collective-permute-start | bytes 589832 | tf_op jit(solution)/shard_map/while/body/eval_jaxpr/ppermute | solution.py:16
  159.7 14.9 %collective-permute-start.1 = (bf16[1,128,768]{1,2,0:T(8,128)(2,1)S(1)}, bf16[1,128,768]{1,2,0:T(8,128)(2,1)}, u32[]{:S(2)}, u32[]{:S(2)}) collective-permute-start(bf16[1,128,768]{1,2,0:T(8,128)(2,1)S(1)} %copy.86), channel_id=1, source_target_pairs={{0,1},{1,2},{2,3},{3,0},{4,5},{5,6},{6,7},{7,4},{8,9},{9,10},{10,1... | collective-permute-start | bytes 589832 | tf_op jit(solution)/shard_map/while/body/eval_jaxpr/ppermute | solution.py:16
  167.5 4.1 collective-permute-start.2
  169.5 4.1 collective-permute-start.3
  203.2 6.7 copy-start.53
  209.9 17.0 %copy-start.51 = (bf16[768]{0:T(1024)(128)(2,1)S(1)}, bf16[768]{0:T(1024)(128)(2,1)}, u32[]{:S(2)}) copy-start(bf16[768]{0:T(1024)(128)(2,1)} %get-tuple-element.956) | copy-start | bytes 4612
  314.7 524.5 %all-reduce.4.cloned.1.call-start = ((), (), s32[]{:S(2)}) async-start(), calls=%async_computation | async-start | bytes 7087104 | tf_op jit(solution)/shard_map/psum | solution.py:293
  (35 other events, 103.5 us)
Sparse Core Ops, SparseCore 0:
  314.8 441.9 all-reduce.5
  765.8 73.3 all-reduce.3
where the time goes:
time: 884 us; the launch traced here: 875 us
  waiting for transfers between devices  514 us (58%)
  local copies, waits for them, and re-layouts  188 us (21%)
  matrix products  63.4 us (7%)
  other arithmetic  62 us (7%)
  blocking collectives  18.3 us (2%)
  between operations  15.1 us (2%)
  starting transfers between devices  13.1 us (1%)
    unnamed x3, waiting for transfers between devices  441 us
    unnamed x140, local copies, waits for them, and re-layouts  98.3 us
    psum x1, waiting for transfers between devices, local(): summed = lax.psum(shares, 'blk').astype(jnp.float32)  68.1 us
    reshape x15, local copies, waits for them, and re-layouts, local(): member.reshape(owners, -1)  33.5 us
    reshape x9, other arithmetic, positions(): return (logical, jnp.take_along_axis(clip_ids, logical, axis=1))  23.9 us
  transfers between devices with their start and end apart: 18, of which 7 were waited for; matrix products, arithmetic and copies ran while one was open for 7% of the time, Pallas kernels for 0%

commit v1 on v0

--- a/solution.py
+++ b/solution.py
@@ -1,13 +1,853 @@
+import functools
+import itertools
+import types
+
 import jax
 import jax.numpy as jnp
 from jax import lax
+from jax.experimental import pallas as pl
+from jax.experimental.pallas import tpu as pltpu
 from jax.sharding import PartitionSpec as P
 
 HEADS = 12
-
-
 EPSILON = 1e-05
 MASKED = -1e30
+F32 = jnp.float32
+BF16 = jnp.bfloat16
+MESH = pl.DeviceIdType.MESH
+TOK = 128
+PIECES = 2
+
+
+def mm(left, right, left_dim, right_dim):
+    return lax.dot_general(
+        left, right, (((left_dim,), (right_dim,)), ((), ())), preferred_element_type=F32
+    )
+
+
+def norm_stats(value):
+    centred = value - jnp.mean(value, axis=-1, keepdims=True)
+    inverse = lax.rsqrt(jnp.mean(centred * centred, axis=-1, keepdims=True) + EPSILON)
+    return centred * inverse, inverse
+
+
+def norm_pull(grad, normed, inverse, gain):
+    scaled = grad * gain
+    return inverse * (
+        scaled
+        - jnp.mean(scaled, axis=-1, keepdims=True)
+        - normed * jnp.mean(scaled * normed, axis=-1, keepdims=True)
+    )
+
+
+def row_of(ref):
+    return ref[...].astype(F32).reshape(1, ref.shape[0])
+
+
+def by_rows(start, count, step, body):
+    @pl.loop(0, count // step)
+    def _(index):
+        body(pl.multiple_of(start + index * step, step))
+
+
+def folded(value):
+    rows, columns = value.shape
+    return jnp.sum(value.reshape(rows // 8, 8, columns), axis=0)
+
+
+def fast_scratch():
+    row, d = 4 * TOK, 768
+    vm = pltpu.VMEM
+    return dict(
+        x_all=vm((row, d), BF16),
+        u_all=vm((row, d), BF16),
+        wab=vm((d, 576), BF16),
+        wb_tile=vm((3, d, 128), BF16),
+        wo=vm((d, d), BF16),
+        w1=vm((d, d), BF16),
+        w2=vm((d, d), BF16),
+        first=vm((row, d), BF16),
+        first_t=vm((d, row), BF16),
+        qh=vm((3, row, 64), BF16),
+        kh=vm((3, row, 64), BF16),
+        vh=vm((3, row, 64), BF16),
+        kt=vm((3, 64, row), BF16),
+        vt=vm((3, 64, row), BF16),
+        mask=vm((row, row), F32),
+        st=vm((row, row), F32),
+        pf=vm((3, row, row), F32),
+        pb=vm((3, row, row), BF16),
+        sg=vm((row, row), BF16),
+        at=vm((d, row), BF16),
+        mid=vm((row, d), F32),
+        second=vm((row, d), BF16),
+        hid=vm((row, d), F32),
+        ga=vm((row, d), F32),
+        act=vm((row, d), BF16),
+        gh=vm((row, d), BF16),
+        part=vm((row, d), F32),
+        part_out=vm((row, d), F32),
+        rs_send=vm((3, 3, TOK, d), BF16),
+        rs_recv=vm((3, 3, TOK, d), BF16),
+        g_mid=vm((TOK, d), F32),
+        gb=vm((row, d), BF16),
+        gbt=vm((row, 256), BF16),
+        go=vm((3, row, 64), BF16),
+        gqkv=vm((row, 576), BF16),
+        c_send=vm((384, d), BF16),
+        c_own=vm((384, d), F32),
+        c_recv=vm((3, 384, d), BF16),
+        c_sum=vm((2, 384, d), BF16),
+        e_buf=vm((8, 96, d), BF16),
+        e_r1=vm((4, 96, d), BF16),
+        e_s1=vm((4, 96, d), BF16),
+        e_r2=vm((3, 96, d), BF16),
+        e_s2=vm((2, 96, d), BF16),
+        wa_buf=vm((8, 96, 512), BF16),
+        wa_r1=vm((4, 96, 512), BF16),
+        wa_s1=vm((4, 96, 512), BF16),
+        wa_r2=vm((3, 96, 512), BF16),
+        wa_s2=vm((2, 96, 512), BF16),
+        wb_buf=vm((8, 96, 256), BF16),
+        wb_r1=vm((4, 96, 256), BF16),
+        wb_s1=vm((4, 96, 256), BF16),
+        wb_r2=vm((3, 96, 256), BF16),
+        wb_s2=vm((2, 96, 256), BF16),
+        sv=vm((4, 8, d), F32),
+        sv_recv=vm((3, 8, d), F32),
+        local_sem=pltpu.SemaphoreType.DMA((12,)),
+        send_sem=pltpu.SemaphoreType.DMA((96,)),
+        recv_sem=pltpu.SemaphoreType.DMA((96,)),
+    )
+
+
+INPUTS = [
+    "tokens",
+    "early_gain",
+    "early_shift",
+    "query_weight",
+    "query_bias",
+    "key_weight",
+    "value_weight",
+    "value_bias",
+    "output_weight",
+    "output_bias",
+    "late_gain",
+    "late_shift",
+    "expand_weight",
+    "expand_bias",
+    "contract_weight",
+    "contract_bias",
+    "upstream",
+    "clip_ids",
+    "block_order",
+]
+RESULTS = ["block_out", "token_grad", "ffc", "eg", "wag", "wbg", "svg"]
+
+
+def layer_kernel(names, *refs):
+    r = types.SimpleNamespace(**dict(zip(names, refs)))
+    d_model = 768
+    row = 4 * TOK
+    dp, blk = lax.axis_index("dp"), lax.axis_index("blk")
+    core, chip = blk % 2, blk // 2
+    sibling, across = blk + 1 - 2 * core, (blk + 2) % 4
+    y, z = dp % 2, dp // 2
+    z0, z1 = z % 2, z // 2
+    to_core = {"dp": dp, "blk": sibling}
+    to_x = {"dp": dp, "blk": across}
+    to_y = {"dp": dp + 1 - 2 * y, "blk": blk}
+    to_z0 = {"dp": dp + 2 - 4 * z0, "blk": blk}
+    to_z1 = {"dp": (dp + 4) % 8, "blk": blk}
+    peers = (to_core, to_x, to_y, to_z0, to_z1)
+    numbers = itertools.count()
+    sent = []
+
+    def remote(source, target, peer):
+        number = next(numbers)
+        return pltpu.make_async_remote_copy(
+            src_ref=source,
+            dst_ref=target,
+            send_sem=r.send_sem.at[number],
+            recv_sem=r.recv_sem.at[number],
+            device_id=peer,
+            device_id_type=MESH,
+        )
+
+    def send(source, target, peer):
+        copy = remote(source, target, peer)
+        copy.start()
+        sent.append(copy)
+        return copy
+
+    def rows_at(ref, size, base=0):
+        return lambda index: ref.at[pl.ds(pl.multiple_of(base + index * size, size), size)]
+
+    def gather(source, place):
+        over_x = send(source, place(blk), to_x)
+        over_core = send(source, place(blk), to_core)
+        return over_x, over_core, place
+
+    def forward(gathering):
+        over_x, over_core, place = gathering
+        over_x.wait_recv()
+        return send(place(across), place(across), to_core)
+
+    half = 512 + 128 * chip
+    tile_at = pl.ds(pl.multiple_of(128 * blk, 128), 128)
+    half_at = pl.ds(pl.multiple_of(half, 128), 128)
+    ff_at = pl.ds(pl.multiple_of(768 * blk, 128), 768)
+    own_rows = pl.ds(pl.multiple_of(TOK * blk, TOK), TOK)
+    local = [
+        (r.tokens.at[0], r.x_all.at[own_rows]),
+        (r.query_weight.at[:, tile_at], r.wab.at[:, 0:128]),
+        (r.key_weight.at[:, tile_at], r.wab.at[:, 128:256]),
+        (r.value_weight.at[:, tile_at], r.wab.at[:, 256:384]),
+        (r.query_weight.at[:, half_at], r.wb_tile.at[0]),
+        (r.key_weight.at[:, half_at], r.wb_tile.at[1]),
+        (r.value_weight.at[:, half_at], r.wb_tile.at[2]),
+        (r.output_weight, r.wo),
+        (r.upstream.at[0], r.u_all.at[own_rows]),
+        (r.contract_weight.at[ff_at], r.w2),
+        (r.expand_weight.at[:, ff_at], r.w1),
+    ]
+    loads = []
+    for number, (source, target) in enumerate(local):
+        copy = pltpu.make_async_copy(source, target, r.local_sem.at[number])
+        copy.start()
+        loads.append(copy)
+
+    barrier = pltpu.get_barrier_semaphore()
+    for peer in peers:
+        pl.semaphore_signal(barrier, inc=1, device_id=peer, device_id_type=MESH)
+    pl.semaphore_wait(barrier, len(peers))
+
+    tokens_in = gather(r.tokens.at[0], rows_at(r.x_all, TOK))
+    upstream_in = gather(r.upstream.at[0], rows_at(r.u_all, TOK))
+
+    early_gain, early_shift = row_of(r.early_gain), row_of(r.early_shift)
+    late_gain, late_shift = row_of(r.late_gain), row_of(r.late_shift)
+
+    def picked(vector, size, base, width):
+        total = jnp.zeros((1, width), F32)
+        for index in range(4):
+            begin = base + size * index
+            total = total + jnp.where(blk == index, vector[:, begin : begin + width], 0.0)
+        return total
+
+    query_bias, value_bias = row_of(r.query_bias), row_of(r.value_bias)
+    bias_qkv = jnp.concatenate(
+        [
+            picked(query_bias, 128, 0, 128),
+            jnp.zeros((1, 128), F32),
+            picked(value_bias, 128, 0, 128),
+            picked(query_bias, 64, 512, 64),
+            jnp.zeros((1, 64), F32),
+            picked(value_bias, 64, 512, 64),
+        ],
+        axis=1,
+    )
+
+    lane = lax.broadcasted_iota(jnp.int32, (1, TOK), 1)
+    keys_of, low_of = [], []
+    for index in range(4):
+        place = r.block_order[0, index]
+        clip = jnp.zeros((1, TOK), jnp.int32)
+        for other in range(4):
+            clip = clip + jnp.where(
+                place == other, r.clip_ids[0:1, other * TOK : (other + 1) * TOK], 0
+            )
+        low_of.append((clip * row).astype(F32))
+        keys_of.append((clip * row + place * TOK + lane).astype(F32))
+    for key in range(4):
+        column = jnp.broadcast_to(keys_of[key], (TOK, TOK)).T
+        for query in range(4):
+            allowed = (column <= keys_of[query]) & (column >= low_of[query])
+            r.mask[key * TOK : (key + 1) * TOK, query * TOK : (query + 1) * TOK] = jnp.where(
+                allowed, 0.0, MASKED
+            )
+
+    for copy in loads[1:7]:
+        copy.wait()
+    for index in range(3):
+        tile = r.wb_tile[index].astype(F32)
+        piece = jnp.where(core == 1, tile[:, 64:128], tile[:, 0:64])
+        r.wab[:, 384 + 64 * index : 448 + 64 * index] = piece.astype(BF16)
+
+    def early_norm(start):
+        def body(at):
+            normed, _ = norm_stats(r.x_all[pl.ds(at, 32), :].astype(F32))
+            r.first[pl.ds(at, 32), :] = (normed * early_gain + early_shift).astype(BF16)
+
+        by_rows(start, TOK, 32, body)
+
+    def project(start):
+        at = pl.ds(pl.multiple_of(start, 2 * TOK), 2 * TOK)
+        out = mm(r.first[at, :], r.wab[...], 1, 0) + bias_qkv
+        for head, offset, step in ((0, 0, 128), (1, 64, 128), (2, 384, 64)):
+            query = out[:, offset : offset + 64]
+            r.qh[head, at, :] = (query * 0.125).astype(BF16)
+            r.kh[head, at, :] = out[:, offset + step : offset + step + 64].astype(BF16)
+            r.vh[head, at, :] = out[:, offset + 2 * step : offset + 2 * step + 64].astype(BF16)
+
+    loads[0].wait()
+    early_norm(TOK * blk)
+    tokens_in[1].wait_recv()
+    early_norm(TOK * sibling)
+    project(2 * TOK * chip)
+    token_forward = forward(tokens_in)
+    early_norm(TOK * across)
+    token_forward.wait_recv()
+    early_norm(TOK * ((sibling + 2) % 4))
+    project(2 * TOK * (1 - chip))
+
+    def attend(head):
+        r.st[...] = mm(r.kh[head], r.qh[head], 1, 1)
+
+        @pl.loop(0, 4)
+        def _(strip):
+            at = pl.ds(pl.multiple_of(strip * TOK, TOK), TOK)
+            scores = r.st[:, at] + r.mask[:, at]
+            powers = jnp.exp(scores - jnp.max(scores, axis=0, keepdims=True))
+            probs = powers * (1.0 / jnp.sum(powers, axis=0, keepdims=True))
+            r.pf[head, :, at] = probs
+            r.pb[head, :, at] = probs.astype(BF16)
+
+        r.vt[head] = r.vh[head].T
+        return mm(r.vt[head], r.pb[head], 1, 0).astype(BF16)
+
+    pair_at, third_at = rows_at(r.at, 128), rows_at(r.at, 64, 512)
+    start_pair = pl.multiple_of(128 * blk, 128)
+    r.at[pl.ds(start_pair, 64), :] = attend(0)
+    upstream_forward = forward(upstream_in)
+    r.at[pl.ds(start_pair + 64, 64), :] = attend(1)
+    pair_in = gather(pair_at(blk), pair_at)
+    r.at[pl.ds(pl.multiple_of(512 + 64 * blk, 64), 64), :] = attend(2)
+    third_in = gather(third_at(blk), third_at)
+
+    loads[8].wait()
+    loads[9].wait()
+    upstream_in[1].wait_recv()
+    upstream_forward.wait_recv()
+
+    @pl.loop(0, 3)
+    def _(tile):
+        at = pl.ds(pl.multiple_of(tile * 256, 256), 256)
+        r.ga[:, at] = mm(r.u_all[...], r.w2[at, :], 1, 1)
+
+    pair_forward = forward(pair_in)
+    third_forward = forward(third_in)
+    r.first_t[...] = r.first[...].T
+    for head in range(3):
+        r.kt[head] = r.kh[head].T
+    loads[7].wait()
+    loads[10].wait()
+    pair_in[1].wait_recv()
+    third_in[1].wait_recv()
+    pair_forward.wait_recv()
+    third_forward.wait_recv()
+
+    output_bias = row_of(r.output_bias)
+
+    @pl.loop(0, 2)
+    def _(tile):
+        at = pl.ds(pl.multiple_of(tile * 256, 256), 256)
+        r.mid[at, :] = mm(r.at[:, at], r.wo[...], 0, 0)
+
+    def late_norm(at):
+        at = pl.ds(at, 32)
+        middle = r.mid[at, :] + r.x_all[at, :].astype(F32) + output_bias
+        r.mid[at, :] = middle
+        normed, _ = norm_stats(middle)
+        r.second[at, :] = (normed * late_gain + late_shift).astype(BF16)
+
+    by_rows(0, row, 32, late_norm)
+
+    @pl.loop(0, 3)
+    def _(tile):
+        at = pl.ds(pl.multiple_of(tile * 256, 256), 256)
+        r.hid[:, at] = mm(r.second[...], r.w1[:, at], 1, 0)
+
+    expand_bias = picked(row_of(r.expand_bias), 768, 0, 768)
+    first_factor = 0.7978845608028654
+    third_factor = 0.044715
+
+    def gelu(at):
+        at = pl.ds(at, 16)
+        hidden = r.hid[at, :] + expand_bias
+        square = hidden * hidden
+        bent = jnp.tanh(first_factor * hidden * (1.0 + third_factor * square))
+        grown = 0.5 * (1.0 + bent)
+        r.act[at, :] = (hidden * grown).astype(BF16)
+        slope = grown + (0.5 * first_factor) * hidden * (1.0 - bent * bent) * (
+            1.0 + (3.0 * third_factor) * square
+        )
+        r.gh[at, :] = (r.ga[at, :] * slope).astype(BF16)
+
+    by_rows(0, row, 16, gelu)
+
+    far = (sibling + 2) % 4
+
+    def scatter_start(number, part):
+        copies = [None, None]
+        for index, block in ((1, far), (0, sibling)):
+            at = pl.ds(pl.multiple_of(block * TOK, TOK), TOK)
+            r.rs_send[number, index] = part[at, :].astype(BF16)
+            copies[index] = send(r.rs_send.at[number, index], r.rs_recv.at[number, index], to_core)
+        return copies
+
+    def scatter_middle(number, part, copies):
+        at = pl.ds(pl.multiple_of(across * TOK, TOK), TOK)
+        copies[1].wait_recv()
+        r.rs_send[number, 2] = (part[at, :] + r.rs_recv[number, 1].astype(F32)).astype(BF16)
+        copies.append(send(r.rs_send.at[number, 2], r.rs_recv.at[number, 2], to_x))
+
+    def scatter_end(copies):
+        copies[0].wait_recv()
+        copies[2].wait_recv()
+
+    def scattered(number, part, at, size):
+        own = pl.ds(pl.multiple_of(blk * TOK + at, size), size)
+        here = pl.ds(at, size)
+        return (
+            part[own, :]
+            + r.rs_recv[number, 0, here, :].astype(F32)
+            + r.rs_recv[number, 2, here, :].astype(F32)
+        )
+
+    @pl.loop(0, 3)
+    def _(tile):
+        at = pl.ds(pl.multiple_of(tile * 256, 256), 256)
+        r.part[:, at] = mm(r.gh[...], r.w1[at, :], 1, 1)
+
+    second_sum = scatter_start(0, r.part)
+
+    def contract_half(which):
+        at = pl.ds(pl.multiple_of(384 * which, 384), 384)
+        return mm(r.act[:, at], r.u_all[...], 0, 0)
+
+    piece = 384 // PIECES
+    r.c_send[...] = contract_half(1 - y).astype(BF16)
+    c_y = [
+        send(r.c_send.at[pl.ds(p * piece, piece)], r.c_recv.at[0, pl.ds(p * piece, piece)], to_y)
+        for p in range(PIECES)
+    ]
+    scatter_middle(0, r.part, second_sum)
+    r.c_own[...] = contract_half(y)
+
+    order = (
+        (1 - z0) + 2 * (1 - z1),
+        (1 - z0) + 2 * z1,
+        z0 + 2 * (1 - z1),
+        z0 + 2 * z1,
+    )
+
+    def y_start(buf, first_recv):
+        return [
+            send(buf.at[2 * order[index] + 1 - y], first_recv.at[index], to_y)
+            for index in range(4)
+        ]
+
+    def added(target, left, right):
+        rows = target.shape[0]
+
+        @pl.loop(0, rows // 32)
+        def _(index):
+            at = pl.ds(pl.multiple_of(index * 32, 32), 32)
+            target[at, :] = (left[at, :].astype(F32) + right[at, :].astype(F32)).astype(target.dtype)
+
+    def y_end(copies, buf, first_recv, first_sum, index):
+        copies[index].wait_recv()
+        added(first_sum.at[index], buf.at[2 * order[index] + y], first_recv.at[index])
+
+    def z0_start(first_sum, second_recv):
+        return [send(first_sum.at[index], second_recv.at[index], to_z0) for index in range(2)]
+
+    def z1_start(copies, first_sum, second_recv, second_sums):
+        copies[0].wait_recv()
+        added(second_sums.at[0], first_sum.at[2], second_recv.at[0])
+        copy = send(second_sums.at[0], second_recv.at[2], to_z1)
+        copies[1].wait_recv()
+        added(second_sums.at[1], first_sum.at[3], second_recv.at[1])
+        return copy
+
+    def z1_end(copy, second_sums, second_recv, target):
+        copy.wait_recv()
+        added(target, second_sums.at[1], second_recv.at[2])
+
+    for which in range(2):
+        block = mm(r.second[:, 384 * which : 384 * (which + 1)], r.gh[...], 0, 0)
+        r.e_buf[4 * which : 4 * which + 4] = block.astype(BF16).reshape(4, 96, d_model)
+    e_y = y_start(r.e_buf, r.e_r1)
+
+    @pl.loop(0, 3)
+    def _(tile):
+        at = pl.ds(pl.multiple_of(tile * 256, 256), 256)
+        r.part_out[:, at] = mm(r.act[...], r.w2[:, at], 1, 0)
+
+    out_sum = scatter_start(1, r.part_out)
+
+    scatter_end(second_sum)
+    own_start = blk * TOK
+    r.sv[0] = jnp.zeros((8, d_model), F32)
+
+    def late_pull(index, carry):
+        gain_sum, shift_sum, output_sum, contract_sum = carry
+        at = pl.multiple_of(index * 32, 32)
+        own = pl.ds(pl.multiple_of(own_start + at, 32), 32)
+        grad = scattered(0, r.part, at, 32)
+        normed, inverse = norm_stats(r.mid[own, :])
+        upstream = r.u_all[own, :].astype(F32)
+        middle = upstream + norm_pull(grad, normed, inverse, late_gain)
+        r.g_mid[pl.ds(at, 32), :] = middle
+        low = middle.astype(BF16)
+        r.gb[own, :] = low
+        return (
+            gain_sum + folded(grad * normed),
+            shift_sum + folded(grad),
+            output_sum + folded(low.astype(F32)),
+            contract_sum + folded(upstream),
+        )
+
+    nothing = jnp.zeros((8, d_model), F32)
+    sums = lax.fori_loop(0, TOK // 32, late_pull, (nothing,) * 4)
+    branch_at = rows_at(r.gb, TOK)
+    branch_in = gather(branch_at(blk), branch_at)
+    for index, value in zip((3, 4, 2, 5), sums):
+        r.sv[0, index : index + 1, :] = jnp.sum(value, axis=0, keepdims=True)
+
+    def expand_sum(index, carry):
+        at = pl.ds(pl.multiple_of(index * 32, 32), 32)
+        return carry + folded(r.gh[at, :].astype(F32))
+
+    r.sv[0, 6:7, :] = jnp.sum(
+        lax.fori_loop(0, row // 32, expand_sum, nothing), axis=0, keepdims=True
+    )
+    branch_forward = forward(branch_in)
+    branch_in[1].wait_recv()
+    branch_forward.wait_recv()
+
+    pair = pl.ds(start_pair, 128)
+    pair_grad = mm(r.gb[...], r.wo[pair, :], 1, 1)
+    r.go[0] = pair_grad[:, 0:64].astype(BF16)
+    r.go[1] = pair_grad[:, 64:128].astype(BF16)
+    third = pl.ds(pl.multiple_of(512 + 64 * blk, 64), 64)
+    r.go[2] = mm(r.gb[...], r.wo[third, :], 1, 1).astype(BF16)
+
+    def attend_back(head, offset, step):
+        r.st[...] = mm(r.vh[head], r.go[head], 1, 1)
+
+        @pl.loop(0, 4)
+        def _(strip):
+            at = pl.ds(pl.multiple_of(strip * TOK, TOK), TOK)
+            probs, grad = r.pf[head, :, at], r.st[:, at]
+            delta = jnp.sum(probs * grad, axis=0, keepdims=True)
+            r.sg[:, at] = (probs * (grad - delta)).astype(BF16)
+
+        query = mm(r.kt[head], r.sg[...], 1, 0) * 0.125
+        r.gqkv[:, offset : offset + 64] = query.T.astype(BF16)
+        r.gqkv[:, offset + step : offset + step + 64] = mm(
+            r.sg[...], r.qh[head], 1, 0
+        ).astype(BF16)
+        r.gqkv[:, offset + 2 * step : offset + 2 * step + 64] = mm(
+            r.pb[head], r.go[head], 1, 0
+        ).astype(BF16)
+
+    attend_back(0, 0, 128)
+    attend_back(1, 64, 128)
+
+    r.gbt[:, 0:128] = r.gb[:, tile_at]
+    r.gbt[:, 128:256] = r.gb[:, half_at]
+    for which in range(2):
+        at = slice(384 * which, 384 * (which + 1))
+        block = mm(r.first_t[at, :], r.gqkv[:, 0:384], 1, 0)
+        blocks = slice(4 * which, 4 * which + 4)
+        r.wa_buf[blocks, :, 0:384] = block.astype(BF16).reshape(4, 96, 384)
+        block = mm(r.at[at, :], r.gbt[...], 1, 0)
+        r.wa_buf[blocks, :, 384:512] = block[:, 0:128].astype(BF16).reshape(4, 96, 128)
+        chosen = jnp.where(core == 1, block[:, 192:256], block[:, 128:192])
+        r.wb_buf[blocks, :, 192:256] = chosen.astype(BF16).reshape(4, 96, 64)
+    wa_y = y_start(r.wa_buf, r.wa_r1)
+
+    root0, root1 = blk % 2, blk // 2
+    keeps0 = z0 == root0
+    keeps1 = z1 == root1
+    for p in range(PIECES):
+        c_y[p].wait_recv()
+        at = pl.ds(p * piece, piece)
+        added(r.c_sum.at[0, at], r.c_own.at[at], r.c_recv.at[0, at])
+    c_z0 = [
+        remote(r.c_sum.at[0, pl.ds(p * piece, piece)], r.c_recv.at[1, pl.ds(p * piece, piece)], to_z0)
+        for p in range(PIECES)
+    ]
+    c_z1 = [
+        remote(r.c_sum.at[1, pl.ds(p * piece, piece)], r.c_recv.at[2, pl.ds(p * piece, piece)], to_z1)
+        for p in range(PIECES)
+    ]
+
+    @pl.when(jnp.logical_not(keeps0))
+    def _():
+        for copy in c_z0:
+            copy.start()
+
+    attend_back(2, 384, 64)
+    for which in range(2):
+        at = slice(384 * which, 384 * (which + 1))
+        block = mm(r.first_t[at, :], r.gqkv[:, 384:576], 1, 0)
+        r.wb_buf[4 * which : 4 * which + 4, :, 0:192] = block.astype(BF16).reshape(4, 96, 192)
+    wb_y = y_start(r.wb_buf, r.wb_r1)
+
+    @pl.loop(0, 3)
+    def _(tile):
+        at = pl.ds(pl.multiple_of(tile * 256, 256), 256)
+        r.part[:, at] = mm(r.gqkv[...], r.wab[at, :], 1, 1)
+
+    first_sum = scatter_start(2, r.part)
+
+    def qkv_sum(index, carry):
+        at = pl.ds(pl.multiple_of(index * 32, 32), 32)
+        return carry + folded(r.gqkv[at, :].astype(F32))
+
+    total = jnp.sum(
+        lax.fori_loop(0, row // 32, qkv_sum, jnp.zeros((8, 576), F32)), axis=0, keepdims=True
+    )
+    r.sv[0, 7:8, 0:384] = total[:, 0:384]
+    r.sv[0, 7:8, 512:704] = total[:, 384:576]
+    scatter_middle(2, r.part, first_sum)
+
+    y_end(e_y, r.e_buf, r.e_r1, r.e_s1, 0)
+    y_end(e_y, r.e_buf, r.e_r1, r.e_s1, 1)
+    e_z0 = z0_start(r.e_s1, r.e_r2)
+
+    @pl.when(keeps0)
+    def _():
+        for p in range(PIECES):
+            c_z0[p].wait_recv()
+            at = pl.ds(p * piece, piece)
+            added(r.c_sum.at[1, at], r.c_sum.at[0, at], r.c_recv.at[1, at])
+
+    @pl.when(jnp.logical_and(keeps0, jnp.logical_not(keeps1)))
+    def _():
+        for copy in c_z1:
+            copy.start()
+
+    scatter_middle(1, r.part_out, out_sum)
+    y_end(e_y, r.e_buf, r.e_r1, r.e_s1, 2)
+    y_end(e_y, r.e_buf, r.e_r1, r.e_s1, 3)
+
+    scatter_end(first_sum)
+
+    def early_pull(index, carry):
+        gain_sum, shift_sum = carry
+        at = pl.multiple_of(index * 32, 32)
+        own = pl.ds(pl.multiple_of(own_start + at, 32), 32)
+        here = pl.ds(at, 32)
+        grad = scattered(2, r.part, at, 32)
+        normed, inverse = norm_stats(r.x_all[own, :].astype(F32))
+        pulled = norm_pull(grad, normed, inverse, early_gain)
+        r.token_grad[here, :] = (r.g_mid[here, :] + pulled).astype(BF16)
+        return gain_sum + folded(grad * normed), shift_sum + folded(grad)
+
+    sums = lax.fori_loop(0, TOK // 32, early_pull, (nothing,) * 2)
+    for index, value in enumerate(sums):
+        r.sv[0, index : index + 1, :] = jnp.sum(value, axis=0, keepdims=True)
+    v_y = send(r.sv.at[0], r.sv_recv.at[0], to_y)
+
+    e_z1 = z1_start(e_z0, r.e_s1, r.e_r2, r.e_s2)
+    for index in range(4):
+        y_end(wa_y, r.wa_buf, r.wa_r1, r.wa_s1, index)
+        if index == 1:
+            wa_z0 = z0_start(r.wa_s1, r.wa_r2)
+
+    scatter_end(out_sum)
+    contract_bias = row_of(r.contract_bias)
+
+    @pl.loop(0, TOK // 32)
+    def _(index):
+        at = pl.multiple_of(index * 32, 32)
+        own = pl.ds(pl.multiple_of(own_start + at, 32), 32)
+        value = scattered(1, r.part_out, at, 32) + r.mid[own, :] + contract_bias
+        r.block_out[pl.ds(at, 32), :] = value.astype(BF16)
+
+    v_y.wait_recv()
+    r.sv[1] = r.sv[0] + r.sv_recv[0]
+    v_z0 = send(r.sv.at[1], r.sv_recv.at[1], to_z0)
+    for index in range(4):
+        y_end(wb_y, r.wb_buf, r.wb_r1, r.wb_s1, index)
+        if index == 1:
+            wb_z0 = z0_start(r.wb_s1, r.wb_r2)
+
+    is_root = z == blk
+    is_across = z == across
+    near_root = z == sibling
+    c_x = [remote(r.ffc.at[pl.ds(p * piece, piece)], r.ffc.at[pl.ds(p * piece, piece)], to_x) for p in range(PIECES)]
+    c_core = [remote(r.ffc.at[pl.ds(p * piece, piece)], r.ffc.at[pl.ds(p * piece, piece)], to_core) for p in range(PIECES)]
+
+    @pl.when(is_root)
+    def _():
+        for p in range(PIECES):
+            c_z1[p].wait_recv()
+            at = pl.ds(p * piece, piece)
+            added(r.ffc.at[at], r.c_sum.at[1, at], r.c_recv.at[2, at])
+            c_x[p].start()
+            c_core[p].start()
+
+    e_at = lambda index: r.eg.at[index]
+    z1_end(e_z1, r.e_s2, r.e_r2, r.eg.at[blk])
+    e_in = gather(e_at(blk), e_at)
+
+    v_z0.wait_recv()
+    r.sv[2] = r.sv[1] + r.sv_recv[1]
+    v_z1 = send(r.sv.at[2], r.sv_recv.at[2], to_z1)
+
+    wa_z1 = z1_start(wa_z0, r.wa_s1, r.wa_r2, r.wa_s2)
+    wb_z1 = z1_start(wb_z0, r.wb_s1, r.wb_r2, r.wb_s2)
+
+    @pl.when(is_across)
+    def _():
+        for p in range(PIECES):
+            c_x[p].wait_recv()
+            c_core[p].start()
+
+    e_forward = forward(e_in)
+
+    v_z1.wait_recv()
+    r.svg[blk] = r.sv[2] + r.sv_recv[2]
+    v_at = lambda index: r.svg.at[index]
+    v_in = gather(v_at(blk), v_at)
+
+    wa_at = lambda index: r.wag.at[index]
+    z1_end(wa_z1, r.wa_s2, r.wa_r2, r.wag.at[blk])
+    wa_in = gather(wa_at(blk), wa_at)
+    wb_at = lambda index: r.wbg.at[index]
+    z1_end(wb_z1, r.wb_s2, r.wb_r2, r.wbg.at[blk])
+    wb_in = gather(wb_at(blk), wb_at)
+
+    v_forward = forward(v_in)
+    wa_forward = forward(wa_in)
+    wb_forward = forward(wb_in)
+
+    @pl.when(jnp.logical_not(jnp.logical_or(is_root, is_across)))
+    def _():
+        for p in range(PIECES):
+            c_core[p].wait_recv()
+
+    for gathering in (e_in, v_in, wa_in, wb_in):
+        gathering[1].wait_recv()
+    for copy in (e_forward, v_forward, wa_forward, wb_forward):
+        copy.wait_recv()
+
+    for copy in sent:
+        copy.wait_send()
+
+    @pl.when(jnp.logical_not(keeps0))
+    def _():
+        for copy in c_z0:
+            copy.wait_send()
+
+    @pl.when(jnp.logical_and(keeps0, jnp.logical_not(keeps1)))
+    def _():
+        for copy in c_z1:
+            copy.wait_send()
+
+    @pl.when(is_root)
+    def _():
+        for copy in c_x:
+            copy.wait_send()
+
+    @pl.when(jnp.logical_or(is_root, is_across))
+    def _():
+        for copy in c_core:
+            copy.wait_send()
+
+
+def write_kernel(block_in, grad_in, ffc, eg, wag, wbg, svg, *outs):
+    (block_out, token_grad, gain_early, shift_early, query_grad, bias_query, key_grad, value_grad) = outs[:8]
+    (bias_value, output_grad, bias_output, gain_late, shift_late, expand_grad, bias_expand) = outs[8:15]
+    contract_grad, bias_contract = outs[15:]
+    dp = lax.axis_index("dp")
+    block_out[0] = block_in[...]
+    token_grad[0] = grad_in[...]
+    for index in range(4):
+        wide = slice(128 * index, 128 * (index + 1))
+        narrow = slice(512 + 64 * index, 576 + 64 * index)
+        for number, target in enumerate((query_grad, key_grad, value_grad, output_grad)):
+            target[:, wide] = wag[index, :, 128 * number : 128 * (number + 1)].astype(F32)
+            target[:, narrow] = wbg[index, :, 64 * number : 64 * (number + 1)].astype(F32)
+        expand_grad[:, 768 * index : 768 * (index + 1)] = eg[index].astype(F32)
+    contract_grad[...] = ffc[...].astype(F32)
+    summed = svg[0] + svg[1] + svg[2] + svg[3]
+    query_row = jnp.concatenate(
+        [svg[i, 7:8, 0:128] for i in range(4)] + [svg[i, 7:8, 512:576] for i in range(4)], axis=1
+    )
+    value_row = jnp.concatenate(
+        [svg[i, 7:8, 256:384] for i in range(4)] + [svg[i, 7:8, 640:704] for i in range(4)], axis=1
+    )
+    rows = jnp.concatenate([summed[0:6], query_row, value_row], axis=0)
+    turned = pltpu.roll(rows, 768 - 96 * dp, 1)
+    targets = (gain_early, shift_early, bias_output, gain_late, shift_late, bias_contract)
+    for number, target in enumerate(targets + (bias_query, bias_value)):
+        target[...] = turned[number, 0:96]
+    hidden = jnp.zeros((8, 768), F32)
+    for index in range(4):
+        hidden = hidden + jnp.where(dp // 2 == index, svg[index], 0.0)
+    bias_expand[...] = pltpu.roll(hidden, 768 - 384 * (dp % 2), 1)[6, 0:384]
+
+
+def fast_local(*arguments):
+    scratch = fast_scratch()
+    vmem = pl.BlockSpec(memory_space=pltpu.VMEM)
+    away = pl.BlockSpec(memory_space=pl.ANY)
+    large = [
+        "tokens",
+        "query_weight",
+        "key_weight",
+        "value_weight",
+        "output_weight",
+        "expand_weight",
+        "contract_weight",
+        "upstream",
+    ]
+    specs = [away if name in large else vmem for name in INPUTS]
+    specs[-1] = pl.BlockSpec(memory_space=pltpu.SMEM)
+    shape = jax.ShapeDtypeStruct
+    results = (
+        shape((TOK, 768), BF16),
+        shape((TOK, 768), BF16),
+        shape((384, 768), BF16),
+        shape((4, 96, 768), BF16),
+        shape((4, 96, 512), BF16),
+        shape((4, 96, 256), BF16),
+        shape((4, 8, 768), F32),
+    )
+    names = INPUTS + RESULTS + list(scratch)
+    moved = pl.pallas_call(
+        functools.partial(layer_kernel, names),
+        name="layer",
+        out_shape=results,
+        in_specs=specs,
+        out_specs=(vmem,) * len(results),
+        scratch_shapes=list(scratch.values()),
+        compiler_params=pltpu.CompilerParams(
+            collective_id=0, has_side_effects=True, vmem_limit_bytes=56 << 20
+        ),
+    )(*arguments)
+    outs = (
+        [shape((1, TOK, 768), BF16)] * 2
+        + [shape((96,), F32)] * 2
+        + [shape((96, 768), F32), shape((96,), F32), shape((96, 768), F32), shape((96, 768), F32)]
+        + [shape((96,), F32), shape((96, 768), F32)]
+        + [shape((96,), F32)] * 3
+        + [shape((96, 3072), F32), shape((384,), F32), shape((384, 768), F32), shape((96,), F32)]
+    )
+    return pl.pallas_call(
+        write_kernel,
+        name="write",
+        out_shape=tuple(outs),
+        in_specs=[vmem] * 7,
+        out_specs=(vmem,) * len(outs),
+        compiler_params=pltpu.CompilerParams(vmem_limit_bytes=32 << 20),
+    )(*moved)
 
 
 def passed_along(value, axis, steps):
@@ -54,7 +894,7 @@
     return jnp.sum(grad_rows.astype(jnp.float32), axis=(0, 1))
 
 
-def local(
+def general_local(
     tokens,
     early_gain,
     early_shift,
@@ -323,8 +1163,9 @@
         P("dp", None),
         P("dp", None),
     )
+    narrow = mesh.shape["dp"] == 8 and mesh.shape["blk"] == 4
     return jax.shard_map(
-        local,
+        fast_local if narrow else general_local,
         mesh=mesh,
         in_specs=placed,
         out_specs=(

time: 884 us -> 109 us (0.12)
  waiting for transfers between devices: 514 us -> 0 us
  local copies, waits for them, and re-layouts: 188 us -> 6.79 us
  Pallas kernels: 0 us -> 99.1 us
  matrix products: 63.4 us -> 0 us
  other arithmetic: 62 us -> 0 us
  blocking collectives: 18.3 us -> 0 us
  between operations: 15.1 us -> 0.69 us
  starting transfers between devices: 13.1 us -> 0 us
    unnamed x3 -> x0, waiting for transfers between devices: 441 us -> none
    pallas_call x0 -> x2, Pallas kernels: none -> 99.1 us  [the longest x1 97.1 us: fast_local(): pl.pallas_call(functools.partial(layer_kernel, names), name='layer', out_...]
    unnamed x140 -> x14, local copies, waits for them, and re-layouts: 98.3 us -> 6.79 us
    psum x1 -> x0, waiting for transfers between devices: 68.1 us -> none  [local(): summed = lax.psum(shares, 'blk').astype(jnp.float32)]
    dot_general x46 -> x0, matrix products: 63.4 us -> none  [the longest x6 13.9 us: weight_grad(): jnp.einsum('rtd,rte->de', inputs, grad_rows, preferred_element_type=jnp.f...]
    reshape x15 -> x0, local copies, waits for them, and re-layouts: 33.5 us -> none  [local(): member.reshape(owners, -1)]
    convert_element_type x28 -> x0, other arithmetic: 25.3 us -> none  [the longest x1 6.3 us: local(): summed = lax.psum(shares, 'blk').astype(jnp.float32)]
    reshape x9 -> x0, other arithmetic: 23.9 us -> none  [positions(): return (logical, jnp.take_along_axis(clip_ids, logical, axis=1))]
  transfers between devices with their start and end apart: 18 -> 0, of which waited for: 7 -> 0; matrix products, arithmetic and copies ran while one was open for 7% -> 0% of each run, Pallas kernels for 0% -> 0%
where the time goes in v1:
time: 109 us; the launch traced here: 107 us
  Pallas kernels  99.1 us (91%)
  local copies, waits for them, and re-layouts  6.79 us (6%)
    pallas_call x1, Pallas kernels, fast_local(): pl.pallas_call(functools.partial(layer_kernel, names), name='layer', out_...  97.1 us
    unnamed x14, local copies, waits for them, and re-layouts  6.79 us

profile of v1, /device:TPU:3, one launch (start us, length us, event | category | flops | bytes accessed | tf_op | source)
XLA Modules:
  0.0 106.6 jit_solution(1125684523178071767)
XLA Ops:
  0.7 97.1 %layer.1 = (bf16[128,768]{1,0:T(8,128)(2,1)}, bf16[128,768]{1,0:T(8,128)(2,1)}, bf16[384,768]{1,0:T(8,128)(2,1)}, bf16[4,96,768]{2,1,0:T(8,128)(2,1)}, bf16[4,96...) custom-call(bf16[1,128,768]{2,1,0:T(8,128)(2,1)} %refs_0_.1, bf16[768]{0:T(1024)(128)(2,1)} %refs_1_.1, ...), custom_call_target="tpu_custom_call" | custom-call | tf_op jit(solution)/shard_map/layer/pallas_call | solution.py:824
  97.7 0.0 copy-start
  97.7 1.1 copy-done
  98.8 0.0 copy-start.1
  98.8 1.1 copy-done.1
  99.9 0.0 copy-start.2
  99.9 1.0 copy-done.2
  100.9 0.0 copy-start.3
  100.9 0.9 copy-done.3
  101.8 0.0 copy-start.4
  101.8 0.9 copy-done.4
  102.7 0.0 copy-start.5
  102.7 0.9 copy-done.5
  103.6 0.0 copy-start.6
  103.6 0.9 copy-done.6
  104.5 2.1 %write.1 = (bf16[1,128,768]{2,1,0:T(8,128)(2,1)}, bf16[1,128,768]{2,1,0:T(8,128)(2,1)}, f32[96]{0:T(128)}, f32[96]{0:T(128)}, f32[96,768]{1,0:T(8,128)}, /*index...) custom-call(bf16[128,768]{1,0:T(8,128)(2,1)S(1)} %copy-done.3, ...), custom_call_target="tpu_custom_call" | custom-call | tf_op jit(solution)/shard_map/write/pallas_call | solution.py:843
Async XLA Ops:
  97.7 1.1 copy-start
  98.8 1.1 copy-start.1
  99.9 1.0 copy-start.2
  100.9 0.9 copy-start.3
  101.8 0.9 copy-start.4
  102.7 0.9 copy-start.5
  103.6 0.9 copy-start.6

commit v2 on v1

--- a/solution.py
+++ b/solution.py
@@ -44,8 +44,8 @@
     return ref[...].astype(F32).reshape(1, ref.shape[0])
 
 
-def by_rows(start, count, step, body):
-    @pl.loop(0, count // step)
+def by_rows(start, count, step, body, unroll=2):
+    @pl.loop(0, count // step, unroll=unroll)
     def _(index):
         body(pl.multiple_of(start + index * step, step))
 
@@ -53,6 +53,11 @@
 def folded(value):
     rows, columns = value.shape
     return jnp.sum(value.reshape(rows // 8, 8, columns), axis=0)
+
+
+def halving_scratch(name, width):
+    sizes = {"_buf": 8, "_r1": 4, "_s1": 4, "_r2": 3, "_s2": 2}
+    return {name + key: pltpu.VMEM((size, 96, width), BF16) for key, size in sizes.items()}
 
 
 def fast_scratch():
@@ -67,6 +72,7 @@
         w1=vm((d, d), BF16),
         w2=vm((d, d), BF16),
         first=vm((row, d), BF16),
+        normed=vm((row, d), F32),
         first_t=vm((d, row), BF16),
         qh=vm((3, row, 64), BF16),
         kh=vm((3, row, 64), BF16),
@@ -93,31 +99,26 @@
         gb=vm((row, d), BF16),
         gbt=vm((row, 256), BF16),
         go=vm((3, row, 64), BF16),
+        go_pair=vm((row, 128), BF16),
+        go_send=vm((TOK, 512), BF16),
+        third_send=vm((4, TOK, 64), BF16),
         gqkv=vm((row, 576), BF16),
         c_send=vm((384, d), BF16),
         c_own=vm((384, d), F32),
         c_recv=vm((3, 384, d), BF16),
         c_sum=vm((2, 384, d), BF16),
-        e_buf=vm((8, 96, d), BF16),
-        e_r1=vm((4, 96, d), BF16),
-        e_s1=vm((4, 96, d), BF16),
-        e_r2=vm((3, 96, d), BF16),
-        e_s2=vm((2, 96, d), BF16),
-        wa_buf=vm((8, 96, 512), BF16),
-        wa_r1=vm((4, 96, 512), BF16),
-        wa_s1=vm((4, 96, 512), BF16),
-        wa_r2=vm((3, 96, 512), BF16),
-        wa_s2=vm((2, 96, 512), BF16),
-        wb_buf=vm((8, 96, 256), BF16),
-        wb_r1=vm((4, 96, 256), BF16),
-        wb_s1=vm((4, 96, 256), BF16),
-        wb_r2=vm((3, 96, 256), BF16),
-        wb_s2=vm((2, 96, 256), BF16),
+        **halving_scratch("e1", 384),
+        **halving_scratch("e2", 384),
+        **halving_scratch("wa", 512),
+        **halving_scratch("wb", 256),
         sv=vm((4, 8, d), F32),
         sv_recv=vm((3, 8, d), F32),
-        local_sem=pltpu.SemaphoreType.DMA((12,)),
-        send_sem=pltpu.SemaphoreType.DMA((96,)),
-        recv_sem=pltpu.SemaphoreType.DMA((96,)),
+        **{"v_" + name: vm((4 * d if name == "expand_bias" else d,), BF16) for name in VECTORS},
+        v_clip_ids=vm((1, row), jnp.int32),
+        v_block_order=pltpu.SMEM((1, 4), jnp.int32),
+        local_sem=pltpu.SemaphoreType.DMA((24,)),
+        send_sem=pltpu.SemaphoreType.DMA((128,)),
+        recv_sem=pltpu.SemaphoreType.DMA((128,)),
     )
 
 
@@ -142,7 +143,18 @@
     "clip_ids",
     "block_order",
 ]
-RESULTS = ["block_out", "token_grad", "ffc", "eg", "wag", "wbg", "svg"]
+VECTORS = [
+    "early_gain",
+    "early_shift",
+    "query_bias",
+    "value_bias",
+    "output_bias",
+    "late_gain",
+    "late_shift",
+    "expand_bias",
+    "contract_bias",
+]
+RESULTS = ["block_out", "token_grad", "ffc", "e1g", "e2g", "wag", "wbg", "svg"]
 
 
 def layer_kernel(names, *refs):
@@ -159,7 +171,9 @@
     to_y = {"dp": dp + 1 - 2 * y, "blk": blk}
     to_z0 = {"dp": dp + 2 - 4 * z0, "blk": blk}
     to_z1 = {"dp": (dp + 4) % 8, "blk": blk}
-    peers = (to_core, to_x, to_y, to_z0, to_z1)
+    far = (sibling + 2) % 4
+    to_far = {"dp": dp, "blk": far}
+    peers = (to_core, to_x, to_far, to_y, to_z0, to_z1)
     numbers = itertools.count()
     sent = []
 
@@ -211,6 +225,10 @@
         (r.contract_weight.at[ff_at], r.w2),
         (r.expand_weight.at[:, ff_at], r.w1),
     ]
+    local += [
+        (getattr(r, name), getattr(r, "v_" + name))
+        for name in VECTORS + ["clip_ids", "block_order"]
+    ]
     loads = []
     for number, (source, target) in enumerate(local):
         copy = pltpu.make_async_copy(source, target, r.local_sem.at[number])
@@ -225,8 +243,10 @@
     tokens_in = gather(r.tokens.at[0], rows_at(r.x_all, TOK))
     upstream_in = gather(r.upstream.at[0], rows_at(r.u_all, TOK))
 
-    early_gain, early_shift = row_of(r.early_gain), row_of(r.early_shift)
-    late_gain, late_shift = row_of(r.late_gain), row_of(r.late_shift)
+    for copy in loads[11:]:
+        copy.wait()
+    early_gain, early_shift = row_of(r.v_early_gain), row_of(r.v_early_shift)
+    late_gain, late_shift = row_of(r.v_late_gain), row_of(r.v_late_shift)
 
     def picked(vector, size, base, width):
         total = jnp.zeros((1, width), F32)
@@ -235,7 +255,7 @@
             total = total + jnp.where(blk == index, vector[:, begin : begin + width], 0.0)
         return total
 
-    query_bias, value_bias = row_of(r.query_bias), row_of(r.value_bias)
+    query_bias, value_bias = row_of(r.v_query_bias), row_of(r.v_value_bias)
     bias_qkv = jnp.concatenate(
         [
             picked(query_bias, 128, 0, 128),
@@ -251,11 +271,11 @@
     lane = lax.broadcasted_iota(jnp.int32, (1, TOK), 1)
     keys_of, low_of = [], []
     for index in range(4):
-        place = r.block_order[0, index]
+        place = r.v_block_order[0, index]
         clip = jnp.zeros((1, TOK), jnp.int32)
         for other in range(4):
             clip = clip + jnp.where(
-                place == other, r.clip_ids[0:1, other * TOK : (other + 1) * TOK], 0
+                place == other, r.v_clip_ids[0:1, other * TOK : (other + 1) * TOK], 0
             )
         low_of.append((clip * row).astype(F32))
         keys_of.append((clip * row + place * TOK + lane).astype(F32))
@@ -277,9 +297,10 @@
     def early_norm(start):
         def body(at):
             normed, _ = norm_stats(r.x_all[pl.ds(at, 32), :].astype(F32))
+            r.normed[pl.ds(at, 32), :] = normed
             r.first[pl.ds(at, 32), :] = (normed * early_gain + early_shift).astype(BF16)
 
-        by_rows(start, TOK, 32, body)
+        by_rows(start, TOK, 32, body, 4)
 
     def project(start):
         at = pl.ds(pl.multiple_of(start, 2 * TOK), 2 * TOK)
@@ -316,38 +337,43 @@
         r.vt[head] = r.vh[head].T
         return mm(r.vt[head], r.pb[head], 1, 0).astype(BF16)
 
-    pair_at, third_at = rows_at(r.at, 128), rows_at(r.at, 64, 512)
+    places = (
+        lambda index: pl.multiple_of(128 * index, 64),
+        lambda index: pl.multiple_of(128 * index + 64, 64),
+        lambda index: pl.multiple_of(512 + 64 * index, 64),
+    )
+
+    def head_at(head):
+        return lambda index: r.at.at[pl.ds(places[head](index), 64)]
+
+    def attend_and_send(head):
+        r.at[pl.ds(places[head](blk), 64), :] = attend(head)
+        return gather(head_at(head)(blk), head_at(head))
+
     start_pair = pl.multiple_of(128 * blk, 128)
-    r.at[pl.ds(start_pair, 64), :] = attend(0)
+    heads_in = [attend_and_send(0)]
     upstream_forward = forward(upstream_in)
-    r.at[pl.ds(start_pair + 64, 64), :] = attend(1)
-    pair_in = gather(pair_at(blk), pair_at)
-    r.at[pl.ds(pl.multiple_of(512 + 64 * blk, 64), 64), :] = attend(2)
-    third_in = gather(third_at(blk), third_at)
+    heads_in += [attend_and_send(1), attend_and_send(2)]
 
     loads[8].wait()
     loads[9].wait()
     upstream_in[1].wait_recv()
     upstream_forward.wait_recv()
-
-    @pl.loop(0, 3)
-    def _(tile):
-        at = pl.ds(pl.multiple_of(tile * 256, 256), 256)
+    head_forwards = []
+    for tile in range(3):
+        at = slice(256 * tile, 256 * (tile + 1))
         r.ga[:, at] = mm(r.u_all[...], r.w2[at, :], 1, 1)
-
-    pair_forward = forward(pair_in)
-    third_forward = forward(third_in)
+        head_forwards.append(forward(heads_in[tile]))
     r.first_t[...] = r.first[...].T
     for head in range(3):
         r.kt[head] = r.kh[head].T
     loads[7].wait()
     loads[10].wait()
-    pair_in[1].wait_recv()
-    third_in[1].wait_recv()
-    pair_forward.wait_recv()
-    third_forward.wait_recv()
-
-    output_bias = row_of(r.output_bias)
+    for head in range(3):
+        heads_in[head][1].wait_recv()
+        head_forwards[head].wait_recv()
+
+    output_bias = row_of(r.v_output_bias)
 
     @pl.loop(0, 2)
     def _(tile):
@@ -361,14 +387,14 @@
         normed, _ = norm_stats(middle)
         r.second[at, :] = (normed * late_gain + late_shift).astype(BF16)
 
-    by_rows(0, row, 32, late_norm)
+    by_rows(0, row, 32, late_norm, 4)
 
     @pl.loop(0, 3)
     def _(tile):
         at = pl.ds(pl.multiple_of(tile * 256, 256), 256)
         r.hid[:, at] = mm(r.second[...], r.w1[:, at], 1, 0)
 
-    expand_bias = picked(row_of(r.expand_bias), 768, 0, 768)
+    expand_bias = picked(row_of(r.v_expand_bias), 768, 0, 768)
     first_factor = 0.7978845608028654
     third_factor = 0.044715
 
@@ -386,7 +412,14 @@
 
     by_rows(0, row, 16, gelu)
 
-    far = (sibling + 2) % 4
+    def contract_half(which):
+        at = pl.ds(pl.multiple_of(384 * which, 384), 384)
+        return mm(r.act[:, at], r.u_all[...], 0, 0)
+
+    piece = 384 // PIECES
+    pieces = [pl.ds(p * piece, piece) for p in range(PIECES)]
+    r.c_send[...] = contract_half(1 - y).astype(BF16)
+    c_y = [send(r.c_send.at[at], r.c_recv.at[0, at], to_y) for at in pieces]
 
     def scatter_start(number, part):
         copies = [None, None]
@@ -415,70 +448,82 @@
             + r.rs_recv[number, 2, here, :].astype(F32)
         )
 
+    def added(target, left, right):
+        rows = target.shape[0]
+
+        @pl.loop(0, rows // 32)
+        def _(index):
+            at = pl.ds(pl.multiple_of(index * 32, 32), 32)
+            target[at, :] = (left[at, :].astype(F32) + right[at, :].astype(F32)).astype(target.dtype)
+
+    along_y, along_z0, along_z1 = (y, 1, to_y), (z0, 2, to_z0), (z1, 4, to_z1)
+
+    def halving(name, stages):
+        buf, r1, s1, r2, s2 = (
+            getattr(r, name + key) for key in ("_buf", "_r1", "_s1", "_r2", "_s2")
+        )
+        own = [bit * weight for bit, weight, _ in stages]
+        other = [(1 - bit) * weight for bit, weight, _ in stages]
+        rest = [
+            later + last
+            for later in (other[1], own[1])
+            for last in (other[2], own[2])
+        ]
+        copies = {}
+
+        def start1():
+            copies[1] = [
+                send(buf.at[other[0] + rest[index]], r1.at[index], stages[0][2])
+                for index in range(4)
+            ]
+
+        def end1(*indices):
+            for index in indices:
+                copies[1][index].wait_recv()
+                added(s1.at[index], buf.at[own[0] + rest[index]], r1.at[index])
+
+        def start2():
+            copies[2] = [send(s1.at[index], r2.at[index], stages[1][2]) for index in range(2)]
+
+        def start3():
+            copies[2][0].wait_recv()
+            added(s2.at[0], s1.at[2], r2.at[0])
+            copies[3] = send(s2.at[0], r2.at[2], stages[2][2])
+            copies[2][1].wait_recv()
+            added(s2.at[1], s1.at[3], r2.at[1])
+
+        def finish(target):
+            copies[3].wait_recv()
+            added(target.at[blk], s2.at[1], r2.at[2])
+            place = lambda index: target.at[index]
+            return gather(place(blk), place)
+
+        return types.SimpleNamespace(
+            start1=start1, end1=end1, start2=start2, start3=start3, finish=finish
+        )
+
+    e1 = halving("e1", (along_z0, along_z1, along_y))
+    e2 = halving("e2", (along_y, along_z0, along_z1))
+    wa = halving("wa", (along_y, along_z0, along_z1))
+    wb = halving("wb", (along_y, along_z0, along_z1))
+
+    def expand_part(target, columns):
+        for which in range(2):
+            block = mm(r.second[:, 384 * which : 384 * (which + 1)], r.gh[:, columns], 0, 0)
+            target[4 * which : 4 * which + 4] = block.astype(BF16).reshape(4, 96, 384)
+
     @pl.loop(0, 3)
     def _(tile):
         at = pl.ds(pl.multiple_of(tile * 256, 256), 256)
         r.part[:, at] = mm(r.gh[...], r.w1[at, :], 1, 1)
 
     second_sum = scatter_start(0, r.part)
-
-    def contract_half(which):
-        at = pl.ds(pl.multiple_of(384 * which, 384), 384)
-        return mm(r.act[:, at], r.u_all[...], 0, 0)
-
-    piece = 384 // PIECES
-    r.c_send[...] = contract_half(1 - y).astype(BF16)
-    c_y = [
-        send(r.c_send.at[pl.ds(p * piece, piece)], r.c_recv.at[0, pl.ds(p * piece, piece)], to_y)
-        for p in range(PIECES)
-    ]
+    expand_part(r.e1_buf, slice(0, 384))
+    e1.start1()
     scatter_middle(0, r.part, second_sum)
     r.c_own[...] = contract_half(y)
-
-    order = (
-        (1 - z0) + 2 * (1 - z1),
-        (1 - z0) + 2 * z1,
-        z0 + 2 * (1 - z1),
-        z0 + 2 * z1,
-    )
-
-    def y_start(buf, first_recv):
-        return [
-            send(buf.at[2 * order[index] + 1 - y], first_recv.at[index], to_y)
-            for index in range(4)
-        ]
-
-    def added(target, left, right):
-        rows = target.shape[0]
-
-        @pl.loop(0, rows // 32)
-        def _(index):
-            at = pl.ds(pl.multiple_of(index * 32, 32), 32)
-            target[at, :] = (left[at, :].astype(F32) + right[at, :].astype(F32)).astype(target.dtype)
-
-    def y_end(copies, buf, first_recv, first_sum, index):
-        copies[index].wait_recv()
-        added(first_sum.at[index], buf.at[2 * order[index] + y], first_recv.at[index])
-
-    def z0_start(first_sum, second_recv):
-        return [send(first_sum.at[index], second_recv.at[index], to_z0) for index in range(2)]
-
-    def z1_start(copies, first_sum, second_recv, second_sums):
-        copies[0].wait_recv()
-        added(second_sums.at[0], first_sum.at[2], second_recv.at[0])
-        copy = send(second_sums.at[0], second_recv.at[2], to_z1)
-        copies[1].wait_recv()
-        added(second_sums.at[1], first_sum.at[3], second_recv.at[1])
-        return copy
-
-    def z1_end(copy, second_sums, second_recv, target):
-        copy.wait_recv()
-        added(target, second_sums.at[1], second_recv.at[2])
-
-    for which in range(2):
-        block = mm(r.second[:, 384 * which : 384 * (which + 1)], r.gh[...], 0, 0)
-        r.e_buf[4 * which : 4 * which + 4] = block.astype(BF16).reshape(4, 96, d_model)
-    e_y = y_start(r.e_buf, r.e_r1)
+    expand_part(r.e2_buf, slice(384, 768))
+    e2.start1()
 
     @pl.loop(0, 3)
     def _(tile):
@@ -511,11 +556,65 @@
 
     nothing = jnp.zeros((8, d_model), F32)
     sums = lax.fori_loop(0, TOK // 32, late_pull, (nothing,) * 4)
+
+    pulled = mm(r.gb[own_rows, :], r.wo[...], 1, 1)
+    r.go_send[...] = pulled[:, 0:512].astype(BF16)
+    for index in range(4):
+        r.third_send[index] = pulled[:, 512 + 64 * index : 576 + 64 * index].astype(BF16)
+    head_grads = []
+    for block, peer in ((far, to_far), (across, to_x), (sibling, to_core)):
+        lanes = pl.ds(pl.multiple_of(128 * block, 128), 128)
+        head_grads.append(send(r.go_send.at[:, lanes], r.go_pair.at[own_rows], peer))
+        head_grads.append(send(r.third_send.at[block], r.go.at[2, own_rows], peer))
+    r.go_pair[own_rows, :] = r.go_send[:, tile_at]
+    r.go[2, own_rows, :] = r.third_send[blk]
     branch_at = rows_at(r.gb, TOK)
     branch_in = gather(branch_at(blk), branch_at)
     for index, value in zip((3, 4, 2, 5), sums):
         r.sv[0, index : index + 1, :] = jnp.sum(value, axis=0, keepdims=True)
 
+    e1.end1(0, 1)
+    e1.start2()
+
+    root0, root1 = blk % 2, blk // 2
+    keeps0 = z0 == root0
+    keeps1 = z1 == root1
+    is_root = z == blk
+    is_across = z == across
+    c_z0 = [remote(r.c_sum.at[0, at], r.c_recv.at[1, at], to_z0) for at in pieces]
+    c_z1 = [remote(r.c_sum.at[1, at], r.c_recv.at[2, at], to_z1) for at in pieces]
+    c_x = [remote(r.ffc.at[at], r.ffc.at[at], to_x) for at in pieces]
+    c_core = [remote(r.ffc.at[at], r.ffc.at[at], to_core) for at in pieces]
+
+    def contract_y_end(p):
+        c_y[p].wait_recv()
+        added(r.c_sum.at[0, pieces[p]], r.c_own.at[pieces[p]], r.c_recv.at[0, pieces[p]])
+
+        @pl.when(jnp.logical_not(keeps0))
+        def _():
+            c_z0[p].start()
+
+    def contract_z0_end(p):
+        @pl.when(keeps0)
+        def _():
+            c_z0[p].wait_recv()
+            added(r.c_sum.at[1, pieces[p]], r.c_sum.at[0, pieces[p]], r.c_recv.at[1, pieces[p]])
+
+            @pl.when(jnp.logical_not(keeps1))
+            def _():
+                c_z1[p].start()
+
+    def contract_z1_end(p):
+        @pl.when(is_root)
+        def _():
+            c_z1[p].wait_recv()
+            added(r.ffc.at[pieces[p]], r.c_sum.at[1, pieces[p]], r.c_recv.at[2, pieces[p]])
+            c_x[p].start()
+            c_core[p].start()
+
+    contract_y_end(0)
+    e1.end1(2, 3)
+
     def expand_sum(index, carry):
         at = pl.ds(pl.multiple_of(index * 32, 32), 32)
         return carry + folded(r.gh[at, :].astype(F32))
@@ -523,16 +622,10 @@
     r.sv[0, 6:7, :] = jnp.sum(
         lax.fori_loop(0, row // 32, expand_sum, nothing), axis=0, keepdims=True
     )
-    branch_forward = forward(branch_in)
-    branch_in[1].wait_recv()
-    branch_forward.wait_recv()
-
-    pair = pl.ds(start_pair, 128)
-    pair_grad = mm(r.gb[...], r.wo[pair, :], 1, 1)
-    r.go[0] = pair_grad[:, 0:64].astype(BF16)
-    r.go[1] = pair_grad[:, 64:128].astype(BF16)
-    third = pl.ds(pl.multiple_of(512 + 64 * blk, 64), 64)
-    r.go[2] = mm(r.gb[...], r.wo[third, :], 1, 1).astype(BF16)
+    for copy in head_grads:
+        copy.wait_recv()
+    r.go[0] = r.go_pair[:, 0:64]
+    r.go[1] = r.go_pair[:, 64:128]
 
     def attend_back(head, offset, step):
         r.st[...] = mm(r.vh[head], r.go[head], 1, 1)
@@ -554,48 +647,30 @@
         ).astype(BF16)
 
     attend_back(0, 0, 128)
+    branch_forward = forward(branch_in)
     attend_back(1, 64, 128)
-
+    contract_y_end(1)
+    halves = [(slice(4 * w, 4 * w + 4), slice(384 * w, 384 * (w + 1))) for w in range(2)]
+    for blocks, at in halves:
+        block = mm(r.first_t[at, :], r.gqkv[:, 0:384], 1, 0)
+        r.wa_buf[blocks, :, 0:384] = block.astype(BF16).reshape(4, 96, 384)
+    branch_in[1].wait_recv()
+    branch_forward.wait_recv()
     r.gbt[:, 0:128] = r.gb[:, tile_at]
     r.gbt[:, 128:256] = r.gb[:, half_at]
-    for which in range(2):
-        at = slice(384 * which, 384 * (which + 1))
-        block = mm(r.first_t[at, :], r.gqkv[:, 0:384], 1, 0)
-        blocks = slice(4 * which, 4 * which + 4)
-        r.wa_buf[blocks, :, 0:384] = block.astype(BF16).reshape(4, 96, 384)
+    for blocks, at in halves:
         block = mm(r.at[at, :], r.gbt[...], 1, 0)
         r.wa_buf[blocks, :, 384:512] = block[:, 0:128].astype(BF16).reshape(4, 96, 128)
         chosen = jnp.where(core == 1, block[:, 192:256], block[:, 128:192])
         r.wb_buf[blocks, :, 192:256] = chosen.astype(BF16).reshape(4, 96, 64)
-    wa_y = y_start(r.wa_buf, r.wa_r1)
-
-    root0, root1 = blk % 2, blk // 2
-    keeps0 = z0 == root0
-    keeps1 = z1 == root1
-    for p in range(PIECES):
-        c_y[p].wait_recv()
-        at = pl.ds(p * piece, piece)
-        added(r.c_sum.at[0, at], r.c_own.at[at], r.c_recv.at[0, at])
-    c_z0 = [
-        remote(r.c_sum.at[0, pl.ds(p * piece, piece)], r.c_recv.at[1, pl.ds(p * piece, piece)], to_z0)
-        for p in range(PIECES)
-    ]
-    c_z1 = [
-        remote(r.c_sum.at[1, pl.ds(p * piece, piece)], r.c_recv.at[2, pl.ds(p * piece, piece)], to_z1)
-        for p in range(PIECES)
-    ]
-
-    @pl.when(jnp.logical_not(keeps0))
-    def _():
-        for copy in c_z0:
-            copy.start()
-
+    wa.start1()
+    contract_z0_end(0)
+    e1.start3()
     attend_back(2, 384, 64)
-    for which in range(2):
-        at = slice(384 * which, 384 * (which + 1))
+    for blocks, at in halves:
         block = mm(r.first_t[at, :], r.gqkv[:, 384:576], 1, 0)
-        r.wb_buf[4 * which : 4 * which + 4, :, 0:192] = block.astype(BF16).reshape(4, 96, 192)
-    wb_y = y_start(r.wb_buf, r.wb_r1)
+        r.wb_buf[blocks, :, 0:192] = block.astype(BF16).reshape(4, 96, 192)
+    wb.start1()
 
     @pl.loop(0, 3)
     def _(tile):
@@ -605,40 +680,36 @@
     first_sum = scatter_start(2, r.part)
 
     def qkv_sum(index, carry):
+        gain_sum, shift_sum, bias_sum = carry
         at = pl.ds(pl.multiple_of(index * 32, 32), 32)
-        return carry + folded(r.gqkv[at, :].astype(F32))
-
-    total = jnp.sum(
-        lax.fori_loop(0, row // 32, qkv_sum, jnp.zeros((8, 576), F32)), axis=0, keepdims=True
-    )
+        part = r.part[at, :]
+        return (
+            gain_sum + folded(part * r.normed[at, :]),
+            shift_sum + folded(part),
+            bias_sum + folded(r.gqkv[at, :].astype(F32)),
+        )
+
+    sums = lax.fori_loop(
+        0, row // 32, qkv_sum, (nothing, nothing, jnp.zeros((8, 576), F32))
+    )
+    for index in range(2):
+        r.sv[0, index : index + 1, :] = jnp.sum(sums[index], axis=0, keepdims=True)
+    total = jnp.sum(sums[2], axis=0, keepdims=True)
     r.sv[0, 7:8, 0:384] = total[:, 0:384]
     r.sv[0, 7:8, 512:704] = total[:, 384:576]
+    v_y = send(r.sv.at[0], r.sv_recv.at[0], to_y)
     scatter_middle(2, r.part, first_sum)
-
-    y_end(e_y, r.e_buf, r.e_r1, r.e_s1, 0)
-    y_end(e_y, r.e_buf, r.e_r1, r.e_s1, 1)
-    e_z0 = z0_start(r.e_s1, r.e_r2)
-
-    @pl.when(keeps0)
-    def _():
-        for p in range(PIECES):
-            c_z0[p].wait_recv()
-            at = pl.ds(p * piece, piece)
-            added(r.c_sum.at[1, at], r.c_sum.at[0, at], r.c_recv.at[1, at])
-
-    @pl.when(jnp.logical_and(keeps0, jnp.logical_not(keeps1)))
-    def _():
-        for copy in c_z1:
-            copy.start()
-
+    contract_z0_end(1)
+    e2.end1(0, 1)
+    e2.start2()
+    e2.end1(2, 3)
     scatter_middle(1, r.part_out, out_sum)
-    y_end(e_y, r.e_buf, r.e_r1, r.e_s1, 2)
-    y_end(e_y, r.e_buf, r.e_r1, r.e_s1, 3)
+    e2.start3()
 
     scatter_end(first_sum)
 
-    def early_pull(index, carry):
-        gain_sum, shift_sum = carry
+    @pl.loop(0, TOK // 32)
+    def _(index):
         at = pl.multiple_of(index * 32, 32)
         own = pl.ds(pl.multiple_of(own_start + at, 32), 32)
         here = pl.ds(at, 32)
@@ -646,21 +717,25 @@
         normed, inverse = norm_stats(r.x_all[own, :].astype(F32))
         pulled = norm_pull(grad, normed, inverse, early_gain)
         r.token_grad[here, :] = (r.g_mid[here, :] + pulled).astype(BF16)
-        return gain_sum + folded(grad * normed), shift_sum + folded(grad)
-
-    sums = lax.fori_loop(0, TOK // 32, early_pull, (nothing,) * 2)
-    for index, value in enumerate(sums):
-        r.sv[0, index : index + 1, :] = jnp.sum(value, axis=0, keepdims=True)
-    v_y = send(r.sv.at[0], r.sv_recv.at[0], to_y)
-
-    e_z1 = z1_start(e_z0, r.e_s1, r.e_r2, r.e_s2)
-    for index in range(4):
-        y_end(wa_y, r.wa_buf, r.wa_r1, r.wa_s1, index)
-        if index == 1:
-            wa_z0 = z0_start(r.wa_s1, r.wa_r2)
+
+    contract_z1_end(0)
+    wa.end1(0, 1)
+    wa.start2()
+    e1_in = e1.finish(r.e1g)
+    wa.end1(2, 3)
+    contract_z1_end(1)
+    e2_in = e2.finish(r.e2g)
+    v_y.wait_recv()
+    r.sv[1] = r.sv[0] + r.sv_recv[0]
+    v_z0 = send(r.sv.at[1], r.sv_recv.at[1], to_z0)
+    wb.end1(0, 1)
+    wb.start2()
+    wb.end1(2, 3)
+    e1_forward = forward(e1_in)
+    wa.start3()
 
     scatter_end(out_sum)
-    contract_bias = row_of(r.contract_bias)
+    contract_bias = row_of(r.v_contract_bias)
 
     @pl.loop(0, TOK // 32)
     def _(index):
@@ -669,72 +744,33 @@
         value = scattered(1, r.part_out, at, 32) + r.mid[own, :] + contract_bias
         r.block_out[pl.ds(at, 32), :] = value.astype(BF16)
 
-    v_y.wait_recv()
-    r.sv[1] = r.sv[0] + r.sv_recv[0]
-    v_z0 = send(r.sv.at[1], r.sv_recv.at[1], to_z0)
-    for index in range(4):
-        y_end(wb_y, r.wb_buf, r.wb_r1, r.wb_s1, index)
-        if index == 1:
-            wb_z0 = z0_start(r.wb_s1, r.wb_r2)
-
-    is_root = z == blk
-    is_across = z == across
-    near_root = z == sibling
-    c_x = [remote(r.ffc.at[pl.ds(p * piece, piece)], r.ffc.at[pl.ds(p * piece, piece)], to_x) for p in range(PIECES)]
-    c_core = [remote(r.ffc.at[pl.ds(p * piece, piece)], r.ffc.at[pl.ds(p * piece, piece)], to_core) for p in range(PIECES)]
-
-    @pl.when(is_root)
-    def _():
-        for p in range(PIECES):
-            c_z1[p].wait_recv()
-            at = pl.ds(p * piece, piece)
-            added(r.ffc.at[at], r.c_sum.at[1, at], r.c_recv.at[2, at])
-            c_x[p].start()
-            c_core[p].start()
-
-    e_at = lambda index: r.eg.at[index]
-    z1_end(e_z1, r.e_s2, r.e_r2, r.eg.at[blk])
-    e_in = gather(e_at(blk), e_at)
-
-    v_z0.wait_recv()
-    r.sv[2] = r.sv[1] + r.sv_recv[1]
-    v_z1 = send(r.sv.at[2], r.sv_recv.at[2], to_z1)
-
-    wa_z1 = z1_start(wa_z0, r.wa_s1, r.wa_r2, r.wa_s2)
-    wb_z1 = z1_start(wb_z0, r.wb_s1, r.wb_r2, r.wb_s2)
-
     @pl.when(is_across)
     def _():
         for p in range(PIECES):
             c_x[p].wait_recv()
             c_core[p].start()
 
-    e_forward = forward(e_in)
-
+    v_z0.wait_recv()
+    r.sv[2] = r.sv[1] + r.sv_recv[1]
+    v_z1 = send(r.sv.at[2], r.sv_recv.at[2], to_z1)
+    wb.start3()
+    e2_forward = forward(e2_in)
+    wa_in = wa.finish(r.wag)
     v_z1.wait_recv()
     r.svg[blk] = r.sv[2] + r.sv_recv[2]
     v_at = lambda index: r.svg.at[index]
     v_in = gather(v_at(blk), v_at)
-
-    wa_at = lambda index: r.wag.at[index]
-    z1_end(wa_z1, r.wa_s2, r.wa_r2, r.wag.at[blk])
-    wa_in = gather(wa_at(blk), wa_at)
-    wb_at = lambda index: r.wbg.at[index]
-    z1_end(wb_z1, r.wb_s2, r.wb_r2, r.wbg.at[blk])
-    wb_in = gather(wb_at(blk), wb_at)
-
-    v_forward = forward(v_in)
-    wa_forward = forward(wa_in)
-    wb_forward = forward(wb_in)
+    wb_in = wb.finish(r.wbg)
+    forwards = [e1_forward, e2_forward, forward(wa_in), forward(v_in), forward(wb_in)]
 
     @pl.when(jnp.logical_not(jnp.logical_or(is_root, is_across)))
     def _():
         for p in range(PIECES):
             c_core[p].wait_recv()
 
-    for gathering in (e_in, v_in, wa_in, wb_in):
+    for gathering in (e1_in, e2_in, wa_in, v_in, wb_in):
         gathering[1].wait_recv()
-    for copy in (e_forward, v_forward, wa_forward, wb_forward):
+    for copy in forwards:
         copy.wait_recv()
 
     for copy in sent:
@@ -761,7 +797,17 @@
             copy.wait_send()
 
 
-def write_kernel(block_in, grad_in, ffc, eg, wag, wbg, svg, *outs):
+def write_kernel(*refs):
+    sources, outs, held, sem = refs[:8], refs[8:25], refs[25:33], refs[33]
+    copies = [
+        pltpu.make_async_copy(source, target, sem.at[number])
+        for number, (source, target) in enumerate(zip(sources, held))
+    ]
+    for copy in copies:
+        copy.start()
+    for copy in copies:
+        copy.wait()
+    block_in, grad_in, ffc, e1g, e2g, wag, wbg, svg = held
     (block_out, token_grad, gain_early, shift_early, query_grad, bias_query, key_grad, value_grad) = outs[:8]
     (bias_value, output_grad, bias_output, gain_late, shift_late, expand_grad, bias_expand) = outs[8:15]
     contract_grad, bias_contract = outs[15:]
@@ -774,7 +820,8 @@
         for number, target in enumerate((query_grad, key_grad, value_grad, output_grad)):
             target[:, wide] = wag[index, :, 128 * number : 128 * (number + 1)].astype(F32)
             target[:, narrow] = wbg[index, :, 64 * number : 64 * (number + 1)].astype(F32)
-        expand_grad[:, 768 * index : 768 * (index + 1)] = eg[index].astype(F32)
+        expand_grad[:, 768 * index : 768 * index + 384] = e1g[index].astype(F32)
+        expand_grad[:, 768 * index + 384 : 768 * (index + 1)] = e2g[index].astype(F32)
     contract_grad[...] = ffc[...].astype(F32)
     summed = svg[0] + svg[1] + svg[2] + svg[3]
     query_row = jnp.concatenate(
@@ -798,24 +845,13 @@
     scratch = fast_scratch()
     vmem = pl.BlockSpec(memory_space=pltpu.VMEM)
     away = pl.BlockSpec(memory_space=pl.ANY)
-    large = [
-        "tokens",
-        "query_weight",
-        "key_weight",
-        "value_weight",
-        "output_weight",
-        "expand_weight",
-        "contract_weight",
-        "upstream",
-    ]
-    specs = [away if name in large else vmem for name in INPUTS]
-    specs[-1] = pl.BlockSpec(memory_space=pltpu.SMEM)
     shape = jax.ShapeDtypeStruct
     results = (
         shape((TOK, 768), BF16),
         shape((TOK, 768), BF16),
         shape((384, 768), BF16),
-        shape((4, 96, 768), BF16),
+        shape((4, 96, 384), BF16),
+        shape((4, 96, 384), BF16),
         shape((4, 96, 512), BF16),
         shape((4, 96, 256), BF16),
         shape((4, 8, 768), F32),
@@ -825,7 +861,7 @@
         functools.partial(layer_kernel, names),
         name="layer",
         out_shape=results,
-        in_specs=specs,
+        in_specs=[away] * len(INPUTS),
         out_specs=(vmem,) * len(results),
         scratch_shapes=list(scratch.values()),
         compiler_params=pltpu.CompilerParams(
@@ -844,9 +880,11 @@
         write_kernel,
         name="write",
         out_shape=tuple(outs),
-        in_specs=[vmem] * 7,
+        in_specs=[away] * 8,
         out_specs=(vmem,) * len(outs),
-        compiler_params=pltpu.CompilerParams(vmem_limit_bytes=32 << 20),
+        scratch_shapes=[pltpu.VMEM(item.shape, item.dtype) for item in results]
+        + [pltpu.SemaphoreType.DMA((8,))],
+        compiler_params=pltpu.CompilerParams(vmem_limit_bytes=60 << 20),
     )(*moved)
 
 

time: 109 us -> 89.3 us (0.82); the launches traced: 107 us -> 89.2 us
  Pallas kernels: 99.1 us -> 88.3 us
  local copies, waits for them, and re-layouts: 6.79 us -> 0 us
    pallas_call x1, Pallas kernels: 97.1 us -> 84.6 us  [fast_local(): pl.pallas_call(functools.partial(layer_kernel, names), name='layer', out_...]
    unnamed x14 -> x0, local copies, waits for them, and re-layouts: 6.79 us -> none
    pallas_call x1, Pallas kernels: 2.06 us -> 3.78 us  [fast_local(): pl.pallas_call(write_kernel, name='write', out_shape=tuple(outs), in_spec...]
where the time goes in v2:
time: 89.3 us; the launch traced here: 89.2 us
  Pallas kernels  88.3 us (99%)
    pallas_call x1, Pallas kernels, fast_local(): pl.pallas_call(functools.partial(layer_kernel, names), name='layer', out_...  84.6 us
    pallas_call x1, Pallas kernels, fast_local(): pl.pallas_call(write_kernel, name='write', out_shape=tuple(outs), in_spec...  3.78 us

profile of v2, /device:TPU:3, one launch (start us, length us, event | category | flops | bytes accessed | tf_op | source)
XLA Modules:
  0.0 89.2 jit_solution(1665489676248428958)
XLA Ops:
  0.7 84.6 %layer.1 = (bf16[128,768]{1,0:T(8,128)(2,1)}, bf16[128,768]{1,0:T(8,128)(2,1)}, bf16[384,768]{1,0:T(8,128)(2,1)}, bf16[4,96,384]{2,1,0:T(8,128)(2,1)}, bf16[4,96...) custom-call(bf16[1,128,768]{2,1,0:T(8,128)(2,1)} %refs_0_.1, ...), custom_call_target="tpu_custom_call" | custom-call | tf_op jit(solution)/shard_map/layer/pallas_call | solution.py:860
  85.2 3.8 %write.1 = (bf16[1,128,768]{2,1,0:T(8,128)(2,1)}, bf16[1,128,768]{2,1,0:T(8,128)(2,1)}, f32[96]{0:T(128)}, f32[96]{0:T(128)}, f32[96,768]{1,0:T(8,128)}, /*index...) custom-call(bf16[128,768]{1,0:T(8,128)(2,1)} %get-tuple-element.25.r, ...), custom_call_target="tpu_custom_call" | custom-call | tf_op jit(solution)/shard_map/write/pallas_call | solution.py:879

commit v3 on v2

--- a/solution.py
+++ b/solution.py
@@ -109,14 +109,22 @@
         c_sum=vm((2, 384, d), BF16),
         **halving_scratch("e1", 384),
         **halving_scratch("e2", 384),
-        **halving_scratch("wa", 512),
-        **halving_scratch("wb", 256),
+        **halving_scratch("wa", 384),
+        **halving_scratch("wb", 384),
         sv=vm((4, 8, d), F32),
         sv_recv=vm((3, 8, d), F32),
         **{"v_" + name: vm((4 * d if name == "expand_bias" else d,), BF16) for name in VECTORS},
         v_clip_ids=vm((1, row), jnp.int32),
         v_block_order=pltpu.SMEM((1, 4), jnp.int32),
-        local_sem=pltpu.SemaphoreType.DMA((24,)),
+        block_out=vm((TOK, d), BF16),
+        token_grad=vm((TOK, d), BF16),
+        ffc=vm((384, d), BF16),
+        e1g=vm((4, 96, 384), BF16),
+        e2g=vm((4, 96, 384), BF16),
+        wag=vm((4, 96, 384), BF16),
+        wbg=vm((4, 96, 384), BF16),
+        svg=vm((4, 8, d), F32),
+        local_sem=pltpu.SemaphoreType.DMA((32,)),
         send_sem=pltpu.SemaphoreType.DMA((128,)),
         recv_sem=pltpu.SemaphoreType.DMA((128,)),
     )
@@ -179,6 +187,7 @@
 
     def remote(source, target, peer):
         number = next(numbers)
+        assert number < 128
         return pltpu.make_async_remote_copy(
             src_ref=source,
             dst_ref=target,
@@ -206,6 +215,15 @@
         over_x, over_core, place = gathering
         over_x.wait_recv()
         return send(place(across), place(across), to_core)
+
+    written = []
+
+    def write_out(name):
+        copy = pltpu.make_async_copy(
+            getattr(r, name), getattr(r, "out_" + name), r.local_sem.at[24 + len(written)]
+        )
+        copy.start()
+        written.append(copy)
 
     half = 512 + 128 * chip
     tile_at = pl.ds(pl.multiple_of(128 * blk, 128), 128)
@@ -389,9 +407,8 @@
 
     by_rows(0, row, 32, late_norm, 4)
 
-    @pl.loop(0, 3)
-    def _(tile):
-        at = pl.ds(pl.multiple_of(tile * 256, 256), 256)
+    for tile in range(3):
+        at = slice(256 * tile, 256 * (tile + 1))
         r.hid[:, at] = mm(r.second[...], r.w1[:, at], 1, 0)
 
     expand_bias = picked(row_of(r.v_expand_bias), 768, 0, 768)
@@ -418,15 +435,38 @@
 
     piece = 384 // PIECES
     pieces = [pl.ds(p * piece, piece) for p in range(PIECES)]
+
     r.c_send[...] = contract_half(1 - y).astype(BF16)
     c_y = [send(r.c_send.at[at], r.c_recv.at[0, at], to_y) for at in pieces]
+
+    def block_rows(block):
+        return pl.ds(pl.multiple_of(block * TOK, TOK), TOK)
+
+    def two_blocks(ref, first, second):
+        return jnp.concatenate([ref[block_rows(first), :], ref[block_rows(second), :]], axis=0)
+
+    def scatter_send(number, index):
+        return send(r.rs_send.at[number, index], r.rs_recv.at[number, index], to_core)
+
+    def part_pair(grads, weight, first, second):
+        @pl.loop(0, 3)
+        def _(tile):
+            at = pl.ds(pl.multiple_of(tile * 256, 256), 256)
+            value = mm(two_blocks(grads, first, second), weight[at, :], 1, 1)
+            r.part[block_rows(first), at] = value[0:TOK]
+            r.part[block_rows(second), at] = value[TOK : 2 * TOK]
+
+    def part_start(number, grads, weight):
+        part_pair(grads, weight, far, sibling)
+        copies = scatter_start(number, r.part)
+        part_pair(grads, weight, across, blk)
+        return copies
 
     def scatter_start(number, part):
         copies = [None, None]
         for index, block in ((1, far), (0, sibling)):
-            at = pl.ds(pl.multiple_of(block * TOK, TOK), TOK)
-            r.rs_send[number, index] = part[at, :].astype(BF16)
-            copies[index] = send(r.rs_send.at[number, index], r.rs_recv.at[number, index], to_core)
+            r.rs_send[number, index] = part[block_rows(block), :].astype(BF16)
+            copies[index] = scatter_send(number, index)
         return copies
 
     def scatter_middle(number, part, copies):
@@ -512,22 +552,16 @@
             block = mm(r.second[:, 384 * which : 384 * (which + 1)], r.gh[:, columns], 0, 0)
             target[4 * which : 4 * which + 4] = block.astype(BF16).reshape(4, 96, 384)
 
-    @pl.loop(0, 3)
-    def _(tile):
-        at = pl.ds(pl.multiple_of(tile * 256, 256), 256)
-        r.part[:, at] = mm(r.gh[...], r.w1[at, :], 1, 1)
-
-    second_sum = scatter_start(0, r.part)
+    second_sum = part_start(0, r.gh, r.w1)
+    scatter_middle(0, r.part, second_sum)
     expand_part(r.e1_buf, slice(0, 384))
     e1.start1()
-    scatter_middle(0, r.part, second_sum)
     r.c_own[...] = contract_half(y)
     expand_part(r.e2_buf, slice(384, 768))
     e2.start1()
 
-    @pl.loop(0, 3)
-    def _(tile):
-        at = pl.ds(pl.multiple_of(tile * 256, 256), 256)
+    for tile in range(3):
+        at = slice(256 * tile, 256 * (tile + 1))
         r.part_out[:, at] = mm(r.act[...], r.w2[:, at], 1, 0)
 
     out_sum = scatter_start(1, r.part_out)
@@ -612,8 +646,8 @@
             c_x[p].start()
             c_core[p].start()
 
+    e1.end1(2, 3)
     contract_y_end(0)
-    e1.end1(2, 3)
 
     def expand_sum(index, carry):
         at = pl.ds(pl.multiple_of(index * 32, 32), 32)
@@ -646,38 +680,22 @@
             r.pb[head], r.go[head], 1, 0
         ).astype(BF16)
 
+    halves = [(slice(4 * w, 4 * w + 4), slice(384 * w, 384 * (w + 1))) for w in range(2)]
     attend_back(0, 0, 128)
-    branch_forward = forward(branch_in)
+    contract_y_end(1)
+    contract_z0_end(0)
     attend_back(1, 64, 128)
-    contract_y_end(1)
-    halves = [(slice(4 * w, 4 * w + 4), slice(384 * w, 384 * (w + 1))) for w in range(2)]
     for blocks, at in halves:
         block = mm(r.first_t[at, :], r.gqkv[:, 0:384], 1, 0)
-        r.wa_buf[blocks, :, 0:384] = block.astype(BF16).reshape(4, 96, 384)
-    branch_in[1].wait_recv()
-    branch_forward.wait_recv()
-    r.gbt[:, 0:128] = r.gb[:, tile_at]
-    r.gbt[:, 128:256] = r.gb[:, half_at]
-    for blocks, at in halves:
-        block = mm(r.at[at, :], r.gbt[...], 1, 0)
-        r.wa_buf[blocks, :, 384:512] = block[:, 0:128].astype(BF16).reshape(4, 96, 128)
-        chosen = jnp.where(core == 1, block[:, 192:256], block[:, 128:192])
-        r.wb_buf[blocks, :, 192:256] = chosen.astype(BF16).reshape(4, 96, 64)
+        r.wa_buf[blocks] = block.astype(BF16).reshape(4, 96, 384)
     wa.start1()
-    contract_z0_end(0)
+    scatter_middle(1, r.part_out, out_sum)
+    branch_forward = forward(branch_in)
     e1.start3()
     attend_back(2, 384, 64)
-    for blocks, at in halves:
-        block = mm(r.first_t[at, :], r.gqkv[:, 384:576], 1, 0)
-        r.wb_buf[blocks, :, 0:192] = block.astype(BF16).reshape(4, 96, 192)
-    wb.start1()
-
-    @pl.loop(0, 3)
-    def _(tile):
-        at = pl.ds(pl.multiple_of(tile * 256, 256), 256)
-        r.part[:, at] = mm(r.gqkv[...], r.wab[at, :], 1, 1)
-
-    first_sum = scatter_start(2, r.part)
+    contract_z0_end(1)
+    e2.end1(0, 1)
+    e2.start2()
 
     def qkv_sum(index, carry):
         gain_sum, shift_sum, bias_sum = carry
@@ -689,6 +707,8 @@
             bias_sum + folded(r.gqkv[at, :].astype(F32)),
         )
 
+    first_sum = part_start(2, r.gqkv, r.wab)
+    scatter_middle(2, r.part, first_sum)
     sums = lax.fori_loop(
         0, row // 32, qkv_sum, (nothing, nothing, jnp.zeros((8, 576), F32))
     )
@@ -698,12 +718,39 @@
     r.sv[0, 7:8, 0:384] = total[:, 0:384]
     r.sv[0, 7:8, 512:704] = total[:, 384:576]
     v_y = send(r.sv.at[0], r.sv_recv.at[0], to_y)
-    scatter_middle(2, r.part, first_sum)
-    contract_z0_end(1)
-    e2.end1(0, 1)
-    e2.start2()
+
+    branch_in[1].wait_recv()
+    branch_forward.wait_recv()
+    r.gbt[:, 0:128] = r.gb[:, tile_at]
+    r.gbt[:, 128:256] = r.gb[:, half_at]
+    for blocks, at in halves:
+        block = mm(r.first_t[at, :], r.gqkv[:, 384:576], 1, 0)
+        r.wb_buf[blocks, :, 0:192] = block.astype(BF16).reshape(4, 96, 192)
+        block = mm(r.at[at, :], r.gbt[...], 1, 0)
+        chosen = jnp.where(core == 1, block[:, 192:256], block[:, 128:192])
+        r.wb_buf[blocks, :, 192:256] = chosen.astype(BF16).reshape(4, 96, 64)
+        r.wb_buf[blocks, :, 256:384] = block[:, 0:128].astype(BF16).reshape(4, 96, 128)
+    wb.start1()
+    contract_z1_end(0)
     e2.end1(2, 3)
-    scatter_middle(1, r.part_out, out_sum)
+
+    scatter_end(out_sum)
+    contract_bias = row_of(r.v_contract_bias)
+
+    @pl.loop(0, TOK // 32)
+    def _(index):
+        at = pl.multiple_of(index * 32, 32)
+        own = pl.ds(pl.multiple_of(own_start + at, 32), 32)
+        value = scattered(1, r.part_out, at, 32) + r.mid[own, :] + contract_bias
+        r.block_out[pl.ds(at, 32), :] = value.astype(BF16)
+
+    write_out("block_out")
+    v_y.wait_recv()
+    r.sv[1] = r.sv[0] + r.sv_recv[0]
+    v_z0 = send(r.sv.at[1], r.sv_recv.at[1], to_z0)
+    wa.end1(0, 1)
+    wa.start2()
+    wa.end1(2, 3)
     e2.start3()
 
     scatter_end(first_sum)
@@ -718,31 +765,17 @@
         pulled = norm_pull(grad, normed, inverse, early_gain)
         r.token_grad[here, :] = (r.g_mid[here, :] + pulled).astype(BF16)
 
-    contract_z1_end(0)
-    wa.end1(0, 1)
-    wa.start2()
+    write_out("token_grad")
     e1_in = e1.finish(r.e1g)
-    wa.end1(2, 3)
+    v_z0.wait_recv()
+    r.sv[2] = r.sv[1] + r.sv_recv[1]
+    v_z1 = send(r.sv.at[2], r.sv_recv.at[2], to_z1)
     contract_z1_end(1)
-    e2_in = e2.finish(r.e2g)
-    v_y.wait_recv()
-    r.sv[1] = r.sv[0] + r.sv_recv[0]
-    v_z0 = send(r.sv.at[1], r.sv_recv.at[1], to_z0)
     wb.end1(0, 1)
     wb.start2()
     wb.end1(2, 3)
-    e1_forward = forward(e1_in)
+    e2_in = e2.finish(r.e2g)
     wa.start3()
-
-    scatter_end(out_sum)
-    contract_bias = row_of(r.v_contract_bias)
-
-    @pl.loop(0, TOK // 32)
-    def _(index):
-        at = pl.multiple_of(index * 32, 32)
-        own = pl.ds(pl.multiple_of(own_start + at, 32), 32)
-        value = scattered(1, r.part_out, at, 32) + r.mid[own, :] + contract_bias
-        r.block_out[pl.ds(at, 32), :] = value.astype(BF16)
 
     @pl.when(is_across)
     def _():
@@ -750,28 +783,38 @@
             c_x[p].wait_recv()
             c_core[p].start()
 
-    v_z0.wait_recv()
-    r.sv[2] = r.sv[1] + r.sv_recv[1]
-    v_z1 = send(r.sv.at[2], r.sv_recv.at[2], to_z1)
-    wb.start3()
-    e2_forward = forward(e2_in)
-    wa_in = wa.finish(r.wag)
+    e1_forward = forward(e1_in)
     v_z1.wait_recv()
     r.svg[blk] = r.sv[2] + r.sv_recv[2]
     v_at = lambda index: r.svg.at[index]
     v_in = gather(v_at(blk), v_at)
-    wb_in = wb.finish(r.wbg)
-    forwards = [e1_forward, e2_forward, forward(wa_in), forward(v_in), forward(wb_in)]
+    wb.start3()
+    e2_forward = forward(e2_in)
+    wa_in = wa.finish(r.wag)
 
     @pl.when(jnp.logical_not(jnp.logical_or(is_root, is_across)))
     def _():
         for p in range(PIECES):
             c_core[p].wait_recv()
 
-    for gathering in (e1_in, e2_in, wa_in, v_in, wb_in):
+    write_out("ffc")
+    v_forward = forward(v_in)
+    wb_in = wb.finish(r.wbg)
+    wa_forward = forward(wa_in)
+    wb_forward = forward(wb_in)
+    for name, gathering, copy in (
+        ("e1g", e1_in, e1_forward),
+        ("e2g", e2_in, e2_forward),
+        ("svg", v_in, v_forward),
+        ("wag", wa_in, wa_forward),
+        ("wbg", wb_in, wb_forward),
+    ):
         gathering[1].wait_recv()
-    for copy in forwards:
         copy.wait_recv()
+        write_out(name)
+
+    for copy in written:
+        copy.wait()
 
     for copy in sent:
         copy.wait_send()
@@ -798,31 +841,50 @@
 
 
 def write_kernel(*refs):
-    sources, outs, held, sem = refs[:8], refs[8:25], refs[25:33], refs[33]
-    copies = [
-        pltpu.make_async_copy(source, target, sem.at[number])
+    count, sources, outs = len(RESULTS), refs[: len(RESULTS)], refs[len(RESULTS) :][:17]
+    held, made = refs[count + 17 :][:count], refs[2 * count + 17 :][:15]
+    in_sem, out_sem = refs[-2:]
+    (gain_early, shift_early, query_grad, bias_query, key_grad, value_grad) = made[:6]
+    (bias_value, output_grad, bias_output, gain_late, shift_late, expand_grad, bias_expand) = made[6:13]
+    contract_grad, bias_contract = made[13:]
+    dp = lax.axis_index("dp")
+    loads = [
+        pltpu.make_async_copy(source, target, in_sem.at[number])
         for number, (source, target) in enumerate(zip(sources, held))
     ]
-    for copy in copies:
+    for number in (3, 4, 2, 5, 6, 7, 0, 1):
+        loads[number].start()
+    block_out, token_grad, ffc, e1g, e2g, wag, wbg, svg = held
+    left = []
+
+    def leave(target):
+        number = [item is target for item in made].index(True)
+        copy = pltpu.make_async_copy(target, outs[number + 2], out_sem.at[number + 2])
         copy.start()
-    for copy in copies:
+        left.append(copy)
+
+    for copy in loads[3:5]:
         copy.wait()
-    block_in, grad_in, ffc, e1g, e2g, wag, wbg, svg = held
-    (block_out, token_grad, gain_early, shift_early, query_grad, bias_query, key_grad, value_grad) = outs[:8]
-    (bias_value, output_grad, bias_output, gain_late, shift_late, expand_grad, bias_expand) = outs[8:15]
-    contract_grad, bias_contract = outs[15:]
-    dp = lax.axis_index("dp")
-    block_out[0] = block_in[...]
-    token_grad[0] = grad_in[...]
     for index in range(4):
-        wide = slice(128 * index, 128 * (index + 1))
-        narrow = slice(512 + 64 * index, 576 + 64 * index)
-        for number, target in enumerate((query_grad, key_grad, value_grad, output_grad)):
-            target[:, wide] = wag[index, :, 128 * number : 128 * (number + 1)].astype(F32)
-            target[:, narrow] = wbg[index, :, 64 * number : 64 * (number + 1)].astype(F32)
         expand_grad[:, 768 * index : 768 * index + 384] = e1g[index].astype(F32)
         expand_grad[:, 768 * index + 384 : 768 * (index + 1)] = e2g[index].astype(F32)
+    leave(expand_grad)
+    loads[2].wait()
     contract_grad[...] = ffc[...].astype(F32)
+    leave(contract_grad)
+    for copy in loads[5:7]:
+        copy.wait()
+    for number, target in enumerate((query_grad, key_grad, value_grad, output_grad)):
+        for index in range(4):
+            wide = slice(128 * index, 128 * (index + 1))
+            narrow = slice(512 + 64 * index, 576 + 64 * index)
+            if number < 3:
+                target[:, wide] = wag[index, :, 128 * number : 128 * (number + 1)].astype(F32)
+            else:
+                target[:, wide] = wbg[index, :, 256:384].astype(F32)
+            target[:, narrow] = wbg[index, :, 64 * number : 64 * (number + 1)].astype(F32)
+        leave(target)
+    loads[7].wait()
     summed = svg[0] + svg[1] + svg[2] + svg[3]
     query_row = jnp.concatenate(
         [svg[i, 7:8, 0:128] for i in range(4)] + [svg[i, 7:8, 512:576] for i in range(4)], axis=1
@@ -835,15 +897,23 @@
     targets = (gain_early, shift_early, bias_output, gain_late, shift_late, bias_contract)
     for number, target in enumerate(targets + (bias_query, bias_value)):
         target[...] = turned[number, 0:96]
+        leave(target)
     hidden = jnp.zeros((8, 768), F32)
     for index in range(4):
         hidden = hidden + jnp.where(dp // 2 == index, svg[index], 0.0)
     bias_expand[...] = pltpu.roll(hidden, 768 - 384 * (dp % 2), 1)[6, 0:384]
+    leave(bias_expand)
+    for number, value in enumerate((block_out, token_grad)):
+        loads[number].wait()
+        copy = pltpu.make_async_copy(value, outs[number].at[0], out_sem.at[number])
+        copy.start()
+        left.append(copy)
+    for copy in left:
+        copy.wait()
 
 
 def fast_local(*arguments):
     scratch = fast_scratch()
-    vmem = pl.BlockSpec(memory_space=pltpu.VMEM)
     away = pl.BlockSpec(memory_space=pl.ANY)
     shape = jax.ShapeDtypeStruct
     results = (
@@ -852,17 +922,17 @@
         shape((384, 768), BF16),
         shape((4, 96, 384), BF16),
         shape((4, 96, 384), BF16),
-        shape((4, 96, 512), BF16),
-        shape((4, 96, 256), BF16),
+        shape((4, 96, 384), BF16),
+        shape((4, 96, 384), BF16),
         shape((4, 8, 768), F32),
     )
-    names = INPUTS + RESULTS + list(scratch)
+    names = INPUTS + ["out_" + name for name in RESULTS] + list(scratch)
     moved = pl.pallas_call(
         functools.partial(layer_kernel, names),
         name="layer",
         out_shape=results,
         in_specs=[away] * len(INPUTS),
-        out_specs=(vmem,) * len(results),
+        out_specs=(away,) * len(results),
         scratch_shapes=list(scratch.values()),
         compiler_params=pltpu.CompilerParams(
             collective_id=0, has_side_effects=True, vmem_limit_bytes=56 << 20
@@ -880,10 +950,11 @@
         write_kernel,
         name="write",
         out_shape=tuple(outs),
-        in_specs=[away] * 8,
-        out_specs=(vmem,) * len(outs),
+        in_specs=[away] * len(results),
+        out_specs=(away,) * len(outs),
         scratch_shapes=[pltpu.VMEM(item.shape, item.dtype) for item in results]
-        + [pltpu.SemaphoreType.DMA((8,))],
+        + [pltpu.VMEM(item.shape, item.dtype) for item in outs[2:]]
+        + [pltpu.SemaphoreType.DMA((8,)), pltpu.SemaphoreType.DMA((17,))],
         compiler_params=pltpu.CompilerParams(vmem_limit_bytes=60 << 20),
     )(*moved)
 

time: 89.3 us -> 85.7 us (0.960)
  Pallas kernels: 88.3 us -> 84.5 us
    pallas_call x1, Pallas kernels: 84.6 us -> 81.2 us  [fast_local(): pl.pallas_call(functools.partial(layer_kernel, names), name='layer', out_...]
where the time goes in v3:
time: 85.7 us; the launch traced here: 85.4 us
  Pallas kernels  84.5 us (99%)
    pallas_call x1, Pallas kernels, fast_local(): pl.pallas_call(functools.partial(layer_kernel, names), name='layer', out_...  81.2 us
    pallas_call x1, Pallas kernels, fast_local(): pl.pallas_call(write_kernel, name='write', out_shape=tuple(outs), in_spec...  3.3 us

profile of v3, /device:TPU:3, one launch (start us, length us, event | category | flops | bytes accessed | tf_op | source)
XLA Modules:
  0.0 85.4 jit_solution(2388715225340152147)
XLA Ops:
  0.7 81.2 %layer.1 = (bf16[128,768]{1,0:T(8,128)(2,1)}, bf16[128,768]{1,0:T(8,128)(2,1)}, bf16[384,768]{1,0:T(8,128)(2,1)}, bf16[4,96,384]{2,1,0:T(8,128)(2,1)}, bf16[4,96...) custom-call(bf16[1,128,768]{2,1,0:T(8,128)(2,1)} %refs_0_.1, ...), custom_call_target="tpu_custom_call" | custom-call | tf_op jit(solution)/shard_map/layer/pallas_call | solution.py:930
  81.9 3.3 %write.1 = (bf16[1,128,768]{2,1,0:T(8,128)(2,1)}, bf16[1,128,768]{2,1,0:T(8,128)(2,1)}, f32[96]{0:T(128)}, f32[96]{0:T(128)}, f32[96,768]{1,0:T(8,128)}, /*index...) custom-call(bf16[128,768]{1,0:T(8,128)(2,1)} %get-tuple-element.25.r, ...), custom_call_target="tpu_custom_call" | custom-call | tf_op jit(solution)/shard_map/write/pallas_call | solution.py:949

commit v4 on v3

--- a/solution.py
+++ b/solution.py
@@ -343,7 +343,7 @@
     def attend(head):
         r.st[...] = mm(r.kh[head], r.qh[head], 1, 1)
 
-        @pl.loop(0, 4)
+        @pl.loop(0, 4, unroll=2)
         def _(strip):
             at = pl.ds(pl.multiple_of(strip * TOK, TOK), TOK)
             scores = r.st[:, at] + r.mask[:, at]
@@ -427,7 +427,7 @@
         )
         r.gh[at, :] = (r.ga[at, :] * slope).astype(BF16)
 
-    by_rows(0, row, 16, gelu)
+    by_rows(0, row, 16, gelu, 4)
 
     def contract_half(which):
         at = pl.ds(pl.multiple_of(384 * which, 384), 384)
@@ -491,7 +491,7 @@
     def added(target, left, right):
         rows = target.shape[0]
 
-        @pl.loop(0, rows // 32)
+        @pl.loop(0, rows // 32, unroll=3)
         def _(index):
             at = pl.ds(pl.multiple_of(index * 32, 32), 32)
             target[at, :] = (left[at, :].astype(F32) + right[at, :].astype(F32)).astype(target.dtype)
@@ -589,7 +589,7 @@
         )
 
     nothing = jnp.zeros((8, d_model), F32)
-    sums = lax.fori_loop(0, TOK // 32, late_pull, (nothing,) * 4)
+    sums = lax.fori_loop(0, TOK // 32, late_pull, (nothing,) * 4, unroll=2)
 
     pulled = mm(r.gb[own_rows, :], r.wo[...], 1, 1)
     r.go_send[...] = pulled[:, 0:512].astype(BF16)
@@ -654,7 +654,7 @@
         return carry + folded(r.gh[at, :].astype(F32))
 
     r.sv[0, 6:7, :] = jnp.sum(
-        lax.fori_loop(0, row // 32, expand_sum, nothing), axis=0, keepdims=True
+        lax.fori_loop(0, row // 32, expand_sum, nothing, unroll=4), axis=0, keepdims=True
     )
     for copy in head_grads:
         copy.wait_recv()
@@ -664,7 +664,7 @@
     def attend_back(head, offset, step):
         r.st[...] = mm(r.vh[head], r.go[head], 1, 1)
 
-        @pl.loop(0, 4)
+        @pl.loop(0, 4, unroll=2)
         def _(strip):
             at = pl.ds(pl.multiple_of(strip * TOK, TOK), TOK)
             probs, grad = r.pf[head, :, at], r.st[:, at]
@@ -681,8 +681,8 @@
         ).astype(BF16)
 
     halves = [(slice(4 * w, 4 * w + 4), slice(384 * w, 384 * (w + 1))) for w in range(2)]
+    contract_y_end(1)
     attend_back(0, 0, 128)
-    contract_y_end(1)
     contract_z0_end(0)
     attend_back(1, 64, 128)
     for blocks, at in halves:
@@ -710,7 +710,7 @@
     first_sum = part_start(2, r.gqkv, r.wab)
     scatter_middle(2, r.part, first_sum)
     sums = lax.fori_loop(
-        0, row // 32, qkv_sum, (nothing, nothing, jnp.zeros((8, 576), F32))
+        0, row // 32, qkv_sum, (nothing, nothing, jnp.zeros((8, 576), F32)), unroll=2
     )
     for index in range(2):
         r.sv[0, index : index + 1, :] = jnp.sum(sums[index], axis=0, keepdims=True)
@@ -737,7 +737,7 @@
     scatter_end(out_sum)
     contract_bias = row_of(r.v_contract_bias)
 
-    @pl.loop(0, TOK // 32)
+    @pl.loop(0, TOK // 32, unroll=2)
     def _(index):
         at = pl.multiple_of(index * 32, 32)
         own = pl.ds(pl.multiple_of(own_start + at, 32), 32)
@@ -755,7 +755,7 @@
 
     scatter_end(first_sum)
 
-    @pl.loop(0, TOK // 32)
+    @pl.loop(0, TOK // 32, unroll=2)
     def _(index):
         at = pl.multiple_of(index * 32, 32)
         own = pl.ds(pl.multiple_of(own_start + at, 32), 32)

time: 85.7 us -> 84.9 us (level)
  no operation moved by 1% of the time
where the time goes in v4:
time: 84.9 us; the launch traced here: 84.6 us
  Pallas kernels  83.8 us (99%)
    pallas_call x1, Pallas kernels, fast_local(): pl.pallas_call(functools.partial(layer_kernel, names), name='layer', out_...  80.5 us
    pallas_call x1, Pallas kernels, fast_local(): pl.pallas_call(write_kernel, name='write', out_shape=tuple(outs), in_spec...  3.3 us

profile of v4, /device:TPU:3, one launch (start us, length us, event | category | flops | bytes accessed | tf_op | source)
XLA Modules:
  0.0 84.6 jit_solution(12672212296381748526)
XLA Ops:
  0.7 80.5 %layer.1 = (bf16[128,768]{1,0:T(8,128)(2,1)}, bf16[128,768]{1,0:T(8,128)(2,1)}, bf16[384,768]{1,0:T(8,128)(2,1)}, bf16[4,96,384]{2,1,0:T(8,128)(2,1)}, bf16[4,96...) custom-call(bf16[1,128,768]{2,1,0:T(8,128)(2,1)} %refs_0_.1, ...), custom_call_target="tpu_custom_call" | custom-call | tf_op jit(solution)/shard_map/layer/pallas_call | solution.py:930
  81.1 3.3 %write.1 = (bf16[1,128,768]{2,1,0:T(8,128)(2,1)}, bf16[1,128,768]{2,1,0:T(8,128)(2,1)}, f32[96]{0:T(128)}, f32[96]{0:T(128)}, f32[96,768]{1,0:T(8,128)}, /*index...) custom-call(bf16[128,768]{1,0:T(8,128)(2,1)} %get-tuple-element.25.r, ...), custom_call_target="tpu_custom_call" | custom-call | tf_op jit(solution)/shard_map/write/pallas_call | solution.py:949

commit v5 on v4

--- a/solution.py
+++ b/solution.py
@@ -589,7 +589,7 @@
         )
 
     nothing = jnp.zeros((8, d_model), F32)
-    sums = lax.fori_loop(0, TOK // 32, late_pull, (nothing,) * 4, unroll=2)
+    sums = lax.fori_loop(0, TOK // 32, late_pull, (nothing,) * 4, unroll=4)
 
     pulled = mm(r.gb[own_rows, :], r.wo[...], 1, 1)
     r.go_send[...] = pulled[:, 0:512].astype(BF16)
@@ -710,7 +710,7 @@
     first_sum = part_start(2, r.gqkv, r.wab)
     scatter_middle(2, r.part, first_sum)
     sums = lax.fori_loop(
-        0, row // 32, qkv_sum, (nothing, nothing, jnp.zeros((8, 576), F32)), unroll=2
+        0, row // 32, qkv_sum, (nothing, nothing, jnp.zeros((8, 576), F32)), unroll=4
     )
     for index in range(2):
         r.sv[0, index : index + 1, :] = jnp.sum(sums[index], axis=0, keepdims=True)
@@ -737,7 +737,7 @@
     scatter_end(out_sum)
     contract_bias = row_of(r.v_contract_bias)
 
-    @pl.loop(0, TOK // 32, unroll=2)
+    @pl.loop(0, TOK // 32, unroll=4)
     def _(index):
         at = pl.multiple_of(index * 32, 32)
         own = pl.ds(pl.multiple_of(own_start + at, 32), 32)
@@ -755,7 +755,7 @@
 
     scatter_end(first_sum)
 
-    @pl.loop(0, TOK // 32, unroll=2)
+    @pl.loop(0, TOK // 32, unroll=4)
     def _(index):
         at = pl.multiple_of(index * 32, 32)
         own = pl.ds(pl.multiple_of(own_start + at, 32), 32)

time: 84.9 us -> 84.5 us (level)
  no operation moved by 1% of the time
where the time goes in v5:
time: 84.5 us; the launch traced here: 84.3 us
  Pallas kernels  83.5 us (99%)
    pallas_call x1, Pallas kernels, fast_local(): pl.pallas_call(functools.partial(layer_kernel, names), name='layer', out_...  80.2 us
    pallas_call x1, Pallas kernels, fast_local(): pl.pallas_call(write_kernel, name='write', out_shape=tuple(outs), in_spec...  3.3 us

profile of v5, /device:TPU:3, one launch (start us, length us, event | category | flops | bytes accessed | tf_op | source)
XLA Modules:
  0.0 84.3 jit_solution(13176421057366685783)
XLA Ops:
  0.7 80.2 %layer.1 = (bf16[128,768]{1,0:T(8,128)(2,1)}, bf16[128,768]{1,0:T(8,128)(2,1)}, bf16[384,768]{1,0:T(8,128)(2,1)}, bf16[4,96,384]{2,1,0:T(8,128)(2,1)}, bf16[4,96...) custom-call(bf16[1,128,768]{2,1,0:T(8,128)(2,1)} %refs_0_.1, ...), custom_call_target="tpu_custom_call" | custom-call | tf_op jit(solution)/shard_map/layer/pallas_call | solution.py:930
  80.9 3.3 %write.1 = (bf16[1,128,768]{2,1,0:T(8,128)(2,1)}, bf16[1,128,768]{2,1,0:T(8,128)(2,1)}, f32[96]{0:T(128)}, f32[96]{0:T(128)}, f32[96,768]{1,0:T(8,128)}, /*index...) custom-call(bf16[128,768]{1,0:T(8,128)(2,1)} %get-tuple-element.25.r, ...), custom_call_target="tpu_custom_call" | custom-call | tf_op jit(solution)/shard_map/write/pallas_call | solution.py:949
